TPU v7x, 32 devices: a whole 2x2x4 slice. The times are simulated.
32 devices in a mesh: dp: 4 (over y, x), ctx: 8 (over z, core).
Axes of the slice: x: 2, y: 2, z: 4, core: 2. Of those that a mesh axis runs over, the one named last changes fastest.
Arguments:
- block_input: float32 [4, 1024, 768], P('dp', 'ctx'), may hold values from -6 to 6
- out_cotangent: float32 [4, 1024, 768], P('dp', 'ctx'), may hold values from -6 to 6
- first_gain: float32 [768], replicated, may hold values from 0.25 to 1.75
- first_shift: float32 [768], replicated, may hold values from -3 to 3
- mix_weight: bfloat16 [768, 2304], P('dp'), may hold values from -0.21875 to 0.21875
- query_bias: float32 [768], replicated, may hold values from -3 to 3
- value_bias: float32 [768], replicated, may hold values from -3 to 3
- attn_weight: bfloat16 [768, 768], P('dp'), may hold values from -0.75 to 0.75
- attn_bias: float32 [768], replicated, may hold values from -3 to 3
- second_gain: float32 [768], replicated, may hold values from 0.25 to 1.75
- second_shift: float32 [768], replicated, may hold values from -3 to 3
- up_weight: bfloat16 [768, 3072], P('dp'), may hold values from -0.21875 to 0.21875
- up_bias: float32 [3072], replicated, may hold values from -3 to 3
- down_weight: bfloat16 [3072, 768], P('dp'), may hold values from -0.109375 to 0.109375
- down_bias: float32 [768], replicated, may hold values from -3 to 3
Outputs:
- block_output: float32 [4, 1024, 768], P('dp', 'ctx')
- input_grad: float32 [4, 1024, 768], P('dp', 'ctx')
- first_gain_grad: float32 [768], replicated
- first_shift_grad: float32 [768], replicated
- mix_weight_grad: float32 [768, 2304], P('dp')
- query_bias_grad: float32 [768], replicated
- value_bias_grad: float32 [768], replicated
- attn_weight_grad: float32 [768, 768], P('dp')
- attn_bias_grad: float32 [768], replicated
- second_gain_grad: float32 [768], replicated
- second_shift_grad: float32 [768], replicated
- up_weight_grad: float32 [768, 3072], P('dp')
- up_bias_grad: float32 [3072], replicated
- down_weight_grad: float32 [3072, 768], P('dp')
- down_bias_grad: float32 [768], replicated
All inputs are finite; a program needn't handle non-finite values.
Results may differ from a plain program's by a relative error of at most 0.023.
Values may be sent and summed in bfloat16 or wider, within the bound.
A program may use at most 128 MiB of HBM per device.

v0:
```python
import math

import jax
import jax.numpy as jnp
from jax import lax
from jax.sharding import PartitionSpec as P

H = 12
HD = 64


EPS = 1e-05
GELU_C = math.sqrt(2.0 / math.pi)


def from_behind(value, axis, steps):
    count = lax.axis_size(axis)
    pairs = [(source, (source + steps) % count) for source in range(count)]
    return lax.ppermute(value, axis, pairs)


def layer_norm(x, gain, shift):
    centered = x - jnp.mean(x, axis=-1, keepdims=True)
    rstd = lax.rsqrt(jnp.mean(centered * centered, axis=-1, keepdims=True) + EPS)
    x_hat = centered * rstd
    return (x_hat, rstd, x_hat * gain + shift)


def norm_back(grad, x_hat, rstd, gain):
    g = grad * gain
    return rstd * (
        g
        - jnp.mean(g, axis=-1, keepdims=True)
        - x_hat * jnp.mean(g * x_hat, axis=-1, keepdims=True)
    )


def gelu_pair(u):
    inner = GELU_C * (u + 0.044715 * u * u * u)
    t = jnp.tanh(inner)
    value = 0.5 * u * (1.0 + t)
    slope = 0.5 * (1.0 + t) + 0.5 * u * (1.0 - t * t) * GELU_C * (1.0 + 3.0 * 0.044715 * u * u)
    return (value, slope)


def matmul(a, b):
    return jnp.dot(a, b, preferred_element_type=jnp.float32)


def matmul_tn(a, b):
    return lax.dot_general(a, b, (((0,), (0,)), ((), ())), preferred_element_type=jnp.float32)


def matmul_nt(a, b):
    return lax.dot_general(a, b, (((1,), (1,)), ((), ())), preferred_element_type=jnp.float32)


def body(
    block_input,
    out_cotangent,
    first_gain,
    first_shift,
    mix_weight,
    query_bias,
    value_bias,
    attn_weight,
    attn_bias,
    second_gain,
    second_shift,
    up_weight,
    up_bias,
    down_weight,
    down_bias,
):
    rows = block_input.shape[1]
    width = block_input.shape[2]
    scale = HD ** (-0.5)
    x_rows = block_input.reshape(rows, width)
    cot = out_cotangent.reshape(rows, width)
    mix_full, attn_full, up_full, down_full = (
        lax.all_gather(mix_weight, "dp", axis=0, tiled=True),
        lax.all_gather(attn_weight, "dp", axis=0, tiled=True),
        lax.all_gather(up_weight, "dp", axis=0, tiled=True),
        lax.all_gather(down_weight, "dp", axis=0, tiled=True),
    )
    first_hat, first_rstd, first_out = layer_norm(x_rows, first_gain, first_shift)
    first_in = first_out.astype(jnp.bfloat16)
    mixed = matmul(first_in, mix_full)
    queries = (mixed[:, :width] + query_bias).astype(jnp.bfloat16)
    keys = mixed[:, width : 2 * width].astype(jnp.bfloat16)
    values = (mixed[:, 2 * width :] + value_bias).astype(jnp.bfloat16)
    q3 = queries.reshape(rows, H, HD)
    me = lax.axis_index("ctx")
    cycle_size = lax.axis_size("ctx")
    q_pos = me * rows + jnp.arange(rows)
    q_last = me * rows + rows - 1
    start_state = (
        jnp.full((H, rows), -1e30, jnp.float32),
        jnp.zeros((H, rows), jnp.float32),
        jnp.zeros((H, rows, HD), jnp.float32),
    )
    carry = start_state
    key_piece = lax.all_gather(keys, "ctx", axis=0, tiled=True)
    value_piece = lax.all_gather(values, "ctx", axis=0, tiled=True)
    count = key_piece.shape[0]
    kblock = math.gcd(count, 512)
    nblocks = count // kblock
    key_blocks = key_piece.reshape(nblocks, kblock, H, HD)
    value_blocks = value_piece.reshape(nblocks, kblock, H, HD)
    offsets = jnp.arange(nblocks) * kblock

    def one_block(state, item):
        key_blk, value_blk, offset = item

        def compute(state_in):
            run_max, run_total, run_acc = state_in
            key_pos = offset + jnp.arange(kblock)
            allowed = (key_pos[None, :] <= q_pos[:, None])[None]
            scores = (
                jnp.einsum("qhd,khd->hqk", q3, key_blk, preferred_element_type=jnp.float32) * scale
            )
            scores = jnp.where(allowed, scores, -1e30)
            new_max = jnp.maximum(run_max, jnp.max(scores, axis=-1))
            expo = jnp.where(allowed, jnp.exp(scores - new_max[..., None]), 0.0)
            factor = jnp.exp(run_max - new_max)
            new_total = run_total * factor + jnp.sum(expo, axis=-1)
            new_acc = run_acc * factor[..., None] + jnp.einsum(
                "hqk,khd->hqd", expo, value_blk.astype(jnp.float32), precision=lax.Precision.HIGHEST
            )
            return (new_max, new_total, new_acc)

        def keep_state(state_in):
            return state_in

        return (lax.cond(offset <= q_last, compute, keep_state, state), None)

    carry, unused = lax.scan(one_block, carry, (key_blocks, value_blocks, offsets))
    run_max, run_total, run_acc = carry
    attended = (
        (run_acc / run_total[..., None])
        .transpose(1, 0, 2)
        .reshape(rows, width)
        .astype(jnp.bfloat16)
    )
    lse = run_max + jnp.log(run_total)
    after_attn = x_rows + matmul(attended, attn_full) + attn_bias
    second_hat, second_rstd, second_out = layer_norm(after_attn, second_gain, second_shift)
    second_in = second_out.astype(jnp.bfloat16)
    pre_act = matmul(second_in, up_full) + up_bias
    act_value, act_slope = gelu_pair(pre_act)
    activ = act_value.astype(jnp.bfloat16)
    block_output = after_attn + matmul(activ, down_full) + down_bias
    mix_back, attn_back, up_back, down_back = (
        lax.all_gather(mix_weight, "dp", axis=0, tiled=True),
        lax.all_gather(attn_weight, "dp", axis=0, tiled=True),
        lax.all_gather(up_weight, "dp", axis=0, tiled=True),
        lax.all_gather(down_weight, "dp", axis=0, tiled=True),
    )
    cot_b = cot.astype(jnp.bfloat16)
    down_weight_grad = matmul_tn(activ, cot_b)
    down_bias_grad = jnp.sum(cot, axis=0)
    pre_grad = matmul_nt(cot_b, down_back) * act_slope
    pre_grad_b = pre_grad.astype(jnp.bfloat16)
    up_weight_grad = matmul_tn(second_in, pre_grad_b)
    up_bias_grad = jnp.sum(pre_grad, axis=0)
    second_grad = matmul_nt(pre_grad_b, up_back)
    second_gain_grad = jnp.sum(second_grad * second_hat, axis=0)
    second_shift_grad = jnp.sum(second_grad, axis=0)
    resid_grad = cot + norm_back(second_grad, second_hat, second_rstd, second_gain)
    resid_b = resid_grad.astype(jnp.bfloat16)
    attn_weight_grad = matmul_tn(attended, resid_b)
    attn_bias_grad = jnp.sum(resid_grad, axis=0)
    attended_grad = matmul_nt(resid_b, attn_back).astype(jnp.bfloat16)
    grad3 = attended_grad.reshape(rows, H, HD)
    delta = jnp.sum(
        grad3.astype(jnp.float32) * attended.astype(jnp.float32).reshape(rows, H, HD), axis=-1
    ).T

    def block_grads(key_blk, value_blk, key_start):
        count = key_blk.shape[0]
        key3 = key_blk.reshape(count, H, HD)
        value3 = value_blk.reshape(count, H, HD)
        key_pos = key_start + jnp.arange(count)
        allowed = (key_pos[None, :] <= q_pos[:, None])[None]
        scores = jnp.einsum("qhd,khd->hqk", q3, key3, preferred_element_type=jnp.float32) * scale
        probs = jnp.where(allowed, jnp.exp(scores - lse[..., None]), 0.0)
        dprob = jnp.einsum("qhd,khd->hqk", grad3, value3, preferred_element_type=jnp.float32)
        dscore = probs * (dprob - delta[..., None])
        probs_b = probs.astype(jnp.bfloat16)
        dscore_b = dscore.astype(jnp.bfloat16)
        value_add = jnp.einsum("hqk,qhd->khd", probs_b, grad3, preferred_element_type=jnp.float32)
        key_add = (
            jnp.einsum("hqk,qhd->khd", dscore_b, q3, preferred_element_type=jnp.float32) * scale
        )
        query_add = (
            jnp.einsum("hqk,khd->qhd", dscore_b, key3, preferred_element_type=jnp.float32) * scale
        )
        return (
            query_add.reshape(rows, width),
            key_add.reshape(count, width),
            value_add.reshape(count, width),
        )

    def skip_grads(key_blk, value_blk, key_start):
        count = key_blk.shape[0]
        empty = jnp.zeros((count, width), jnp.float32)
        return (jnp.zeros((rows, width), jnp.float32), empty, empty)

    zeros = jnp.zeros((rows, width), jnp.float32)

    def pass_grads(key_acc, value_acc):
        return (
            from_behind(key_acc.astype(jnp.bfloat16), "ctx", -1).astype(key_acc.dtype),
            from_behind(value_acc.astype(jnp.bfloat16), "ctx", -1).astype(value_acc.dtype),
        )

    def cycle_turn(step, state):
        key_blk, value_blk, key_acc, value_acc, query_acc = state
        owner = (me + step) % cycle_size
        query_add, key_add, value_add = lax.cond(
            owner <= me, block_grads, skip_grads, key_blk, value_blk, owner * rows
        )
        key_blk, value_blk = from_behind((key_blk, value_blk), "ctx", -1)
        key_acc, value_acc = pass_grads(key_acc + key_add, value_acc + value_add)
        return (key_blk, value_blk, key_acc, value_acc, query_acc + query_add)

    key_blk, value_blk, key_acc, value_acc, query_acc = lax.fori_loop(
        0, cycle_size - 1, cycle_turn, (keys, values, zeros, zeros, zeros)
    )
    last_owner = (me + cycle_size - 1) % cycle_size
    query_add, key_add, value_add = lax.cond(
        last_owner <= me, block_grads, skip_grads, key_blk, value_blk, last_owner * rows
    )
    key_grad, value_grad = pass_grads(key_acc + key_add, value_acc + value_add)
    query_grad = query_acc + query_add
    query_bias_grad = jnp.sum(query_grad, axis=0)
    value_bias_grad = jnp.sum(value_grad, axis=0)
    mixed_grad = jnp.concatenate([query_grad, key_grad, value_grad], axis=1).astype(jnp.bfloat16)
    mix_weight_grad = matmul_tn(first_in, mixed_grad)
    first_grad = matmul_nt(mixed_grad, mix_back)
    first_gain_grad = jnp.sum(first_grad * first_hat, axis=0)
    first_shift_grad = jnp.sum(first_grad, axis=0)
    input_grad = resid_grad + norm_back(first_grad, first_hat, first_rstd, first_gain)
    local_mats = (mix_weight_grad, attn_weight_grad, up_weight_grad, down_weight_grad)
    shard_sums = (
        lax.psum_scatter(
            local_mats[0].astype(jnp.bfloat16), "dp", scatter_dimension=0, tiled=True
        ).astype(jnp.float32),
        lax.psum_scatter(
            local_mats[1].astype(jnp.bfloat16), "dp", scatter_dimension=0, tiled=True
        ).astype(jnp.float32),
        lax.psum_scatter(
            local_mats[2].astype(jnp.bfloat16), "dp", scatter_dimension=0, tiled=True
        ).astype(jnp.float32),
        lax.psum_scatter(
            local_mats[3].astype(jnp.bfloat16), "dp", scatter_dimension=0, tiled=True
        ).astype(jnp.float32),
    )
    mats = (
        lax.psum(shard_sums[0].astype(jnp.bfloat16), "ctx").astype(jnp.float32),
        lax.psum(shard_sums[1].astype(jnp.bfloat16), "ctx").astype(jnp.float32),
        lax.psum(shard_sums[2].astype(jnp.bfloat16), "ctx").astype(jnp.float32),
        lax.psum(shard_sums[3].astype(jnp.bfloat16), "ctx").astype(jnp.float32),
    )
    smalls = lax.psum(
        (
            first_gain_grad,
            first_shift_grad,
            query_bias_grad,
            value_bias_grad,
            attn_bias_grad,
            second_gain_grad,
            second_shift_grad,
            up_bias_grad,
            down_bias_grad,
        ),
        ("dp", "ctx"),
    )
    return (
        block_output.reshape(1, rows, width),
        input_grad.reshape(1, rows, width),
        smalls[0],
        smalls[1],
        mats[0],
        smalls[2],
        smalls[3],
        mats[1],
        smalls[4],
        smalls[5],
        smalls[6],
        mats[2],
        smalls[7],
        mats[3],
        smalls[8],
    )


def solution(mesh):
    placed = (
        P("dp", "ctx", None),
        P("dp", "ctx", None),
        P(),
        P(),
        P("dp", None),
        P(),
        P(),
        P("dp", None),
        P(),
        P(),
        P(),
        P("dp", None),
        P(),
        P("dp", None),
        P(),
    )
    return jax.shard_map(
        body,
        mesh=mesh,
        in_specs=placed,
        out_specs=(
            P("dp", "ctx", None),
            P("dp", "ctx", None),
            P(),
            P(),
            P("dp", None),
            P(),
            P(),
            P("dp", None),
            P(),
            P(),
            P(),
            P("dp", None),
            P(),
            P("dp", None),
            P(),
        ),
        check_vma=False,
    )
```

profile of v0, /device:TPU:0, one launch (start us, length us, event | category | flops | bytes accessed | tf_op | source)
XLA Modules:
  0.0 692.6 jit_solution(13095653264918594262)
XLA Ops:
  10.4 49.4 %all-gather.7.cloned.1.call-done = bf16[768,2304]{1,0:T(8,128)(2,1)} async-done(((bf16[192,2304]{1,0:T(8,128)(2,1)}), bf16[768,2304]{1,0:T(8,128)(2,1)}) %all-gather.7.cloned.1.call-update) | async-done | bytes 3538960 | tf_op jit(solution)/shard_map/all_gather | solution.py:81
  67.7 20.9 %all-gather.9.cloned.1.call-done = bf16[1024,768]{1,0:T(8,128)(2,1)} async-done(((bf16[128,768]{1,0:T(8,128)(2,1)}), bf16[1024,768]{1,0:T(8,128)(2,1)}) %all-gather.9.cloned.1.call-update) | async-done | bytes 1572880 | tf_op jit(solution)/shard_map/all_gather | solution.py:103
  94.4 20.8 %all-gather.11.cloned.1.call-done = bf16[1024,768]{1,0:T(8,128)(2,1)} async-done(((bf16[128,768]{1,0:T(8,128)(2,1)}), bf16[1024,768]{1,0:T(8,128)(2,1)}) %all-gather.11.cloned.1.call-update) | async-done | bytes 1572880 | tf_op jit(solution)/shard_map/all_gather | solution.py:104
  125.4 8.6 %while.39 = (s32[]{:T(128)}, f32[12,128]{1,0:T(8,128)S(1)}, f32[12,128]{1,0:T(8,128)S(1)}, f32[12,128,64]{1,2,0:T(8,128)}, s32[2]{0:T(128)S(1)}, /*index=5*/s32[...) while((s32[]{:T(128)}, f32[12,128]{1,0:T(8,128)S(1)}, ...), condition=%wide.region_7.8_spmd.clone, body=%wide.region_2.7_spmd.clone.sunk | while | flops 714346112 | bytes 21801340 | solution.py:137
  126.6 6.1 conditional.8
  135.1 8.6 %all-gather.13.cloned.1.call-done = bf16[768,768]{1,0:T(8,128)(2,1)} async-done(((bf16[192,768]{1,0:T(8,128)(2,1)}), bf16[768,768]{1,0:T(8,128)(2,1)}) %all-gather.13.cloned.1.call-update) | async-done | bytes 1179664 | tf_op jit(solution)/shard_map/all_gather | solution.py:82
  146.2 56.1 %all-gather.15.cloned.1.call-done = bf16[768,3072]{1,0:T(8,128)(2,1)} async-done(((bf16[192,3072]{1,0:T(8,128)(2,1)}), bf16[768,3072]{1,0:T(8,128)(2,1)}) %all-gather.15.cloned.1.call-update) | async-done | bytes 4718608 | tf_op jit(solution)/shard_map/all_gather | solution.py:83
  206.7 54.3 %all-gather.17.cloned.1.call-done = bf16[3072,768]{1,0:T(8,128)(2,1)} async-done(((bf16[768,768]{1,0:T(8,128)(2,1)}), bf16[3072,768]{1,0:T(8,128)(2,1)}) %all-gather.17.cloned.1.call-update) | async-done | bytes 4718608 | tf_op jit(solution)/shard_map/all_gather | solution.py:84
  261.0 5.4 fusion.63
  273.4 132.6 %while.40 = (s32[]{:T(128)}, bf16[128,768]{0,1:T(8,128)(2,1)}, bf16[128,768]{0,1:T(8,128)(2,1)}, f32[128,768]{0,1:T(8,128)S(1)}, f32[128,768]{0,1:T(8,128)S(1)},...) while((s32[]{:T(128)}, bf16[128,768]{0,1:T(8,128)(2,1)}, ...), condition=%wide.region_16.17_spmd.clone, body=%wide.region_13.16_spmd.clone.sunk | while | flops 128401680 | bytes 14401084 | solution.py:227
  280.6 5.2 conditional.9
  300.4 5.1 collective-permute-start.2
  319.4 5.1 collective-permute-start.2
  338.4 5.1 collective-permute-start.2
  357.3 5.1 collective-permute-start.2
  376.3 5.1 collective-permute-start.2
  395.3 5.1 collective-permute-start.2
  406.6 8.9 %collective-permute-start.5 = (bf16[128,768]{0,1:T(8,128)(2,1)S(1)}, bf16[128,768]{0,1:T(8,128)(2,1)S(1)}, u32[]{:S(2)}, u32[]{:S(2)}) collective-permute-start(bf16[128,768]{0,1:T(8,128)(2,1)S(1)} %add_convert_fusion), channel_id=1, source_target_pairs={{0,7},{1,0},{2,1},{3,2},{4,3},{5,4},{6,5},{7,6},{8,15},{9,8},{10,9... | collective-permute-start | bytes 589832 | tf_op jit(solution)/shard_map/ppermute | solution.py:19
  429.7 5.4 convolution_convert_fusion
  435.1 36.4 %reduce-scatter.5.cloned.1.call-done = bf16[192,2304]{1,0:T(8,128)(2,1)} async-done(((bf16[768,2304]{1,0:T(8,128)(2,1)}), bf16[192,2304]{1,0:T(8,128)(2,1)}) %reduce-scatter.5.cloned.1.call-update) | async-done | bytes 884752 | tf_op jit(solution)/shard_map/reduce_scatter | solution.py:246
  471.6 60.0 %reduce-scatter.9.cloned.1.call-done = bf16[192,3072]{1,0:T(8,128)(2,1)} async-done(((bf16[768,3072]{1,0:T(8,128)(2,1)}), bf16[192,3072]{1,0:T(8,128)(2,1)}) %reduce-scatter.9.cloned.1.call-update) | async-done | bytes 1179664 | tf_op jit(solution)/shard_map/reduce_scatter | solution.py:252
  531.6 59.8 %reduce-scatter.11.cloned.1.call-done = bf16[768,768]{1,0:T(8,128)(2,1)} async-done(((bf16[3072,768]{1,0:T(8,128)(2,1)}), bf16[768,768]{1,0:T(8,128)(2,1)}) %reduce-scatter.11.cloned.1.call-update) | async-done | bytes 1179664 | tf_op jit(solution)/shard_map/reduce_scatter | solution.py:255
  598.6 42.0 %all-reduce = (f32[768]{0:T(1024)}, f32[768]{0:T(1024)}, f32[768]{0:T(1024)}, f32[768]{0:T(1024)}, f32[768]{0:T(1024)}, /*index=5*/f32[768]{0:T(1024)}, f32[768]{0:T(1024)}, f32[3072]{0:T(1024)}, f32[768]{0:T(1024)}) all-reduce(f32[768]{0:T(1024)S(1)} %get-tuple-element.662, ...), channel_id=1, replica_groups=mesh['dp'=4,'ctx'=8] {'dp','ctx'}, use_global_device_ids=true, to_apply=%region_22.23 | all-reduce | flops 9216 | bytes 73728 | tf_op jit(solution)/shard_map/psum | solution.py:265
  641.5 37.8 %all-reduce.4.cloned.1.call-done = (bf16[192,2304]{1,0:T(8,128)(2,1)}, bf16[192,768]{1,0:T(8,128)(2,1)}, bf16[192,3072]{1,0:T(8,128)(2,1)}, bf16[768,768]{1,0:T(8,128)(2,1)}) async-done(((bf16[192,2304]{1,0:T(8,128)(2,1)}, bf16[192,768]{1,0:T(8,128)(2,1)}, bf16[192,3072]{1,0:T(8,128)(2,1)}, bf16[768,768]{1,0:T(8,128)(2,1)}), (bf16[192,2304]{1,0:T(8,128)(2,1)}, bf16[192,768]{1,0:T(8,128)(2,1)}, ...) | async-done | bytes 3538960 | tf_op jit(solution)/shard_map/psum | solution.py:260
  (321 shorter events, 180.4 us)
Async XLA Ops:
  7.2 52.5 %all-gather.7.cloned.1.call-start = ((), (), s32[]{:S(2)}) async-start(), calls=%async_computation.4 | async-start | bytes 4423680 | tf_op jit(solution)/shard_map/all_gather | solution.py:81
  7.9 80.7 %all-gather.9.cloned.1.call-start = ((), (), s32[]{:S(2)}) async-start(), calls=%async_computation.5 | async-start | bytes 1769472 | tf_op jit(solution)/shard_map/all_gather | solution.py:103
  63.2 52.1 %all-gather.11.cloned.1.call-start = ((), (), s32[]{:S(2)}) async-start(), calls=%async_computation.6 | async-start | bytes 1769472 | tf_op jit(solution)/shard_map/all_gather | solution.py:104
  64.0 79.7 %all-gather.13.cloned.1.call-start = ((), (), s32[]{:S(2)}) async-start(), calls=%async_computation.7 | async-start | bytes 1474560 | tf_op jit(solution)/shard_map/all_gather | solution.py:82
  64.6 137.7 %all-gather.15.cloned.1.call-start = ((), (), s32[]{:S(2)}) async-start(), calls=%async_computation.8 | async-start | bytes 5898240 | tf_op jit(solution)/shard_map/all_gather | solution.py:83
  65.2 195.8 %all-gather.17.cloned.1.call-start = ((), (), s32[]{:S(2)}) async-start(), calls=%async_computation.9 | async-start | bytes 5898240 | tf_op jit(solution)/shard_map/all_gather | solution.py:84
  65.8 369.4 %reduce-scatter.7.cloned.1.call-start = ((), (), s32[]{:S(2)}) async-start(), calls=%async_computation.11 | async-start | bytes 1474560 | tf_op jit(solution)/shard_map/reduce_scatter | solution.py:249
  273.1 198.4 %reduce-scatter.5.cloned.1.call-start = ((), (), s32[]{:S(2)}) async-start(), calls=%async_computation.10 | async-start | bytes 4423680 | tf_op jit(solution)/shard_map/reduce_scatter | solution.py:246
  275.0 17.1 %collective-permute-start = (bf16[128,768]{0,1:T(8,128)(2,1)}, bf16[128,768]{0,1:T(8,128)(2,1)}, u32[]{:S(2)}, u32[]{:S(2)}) collective-permute-start(bf16[128,768]{0,1:T(8,128)(2,1)} %copy.82), channel_id=1, source_target_pairs={{0,7},{1,0},{2,1},{3,2},{4,3},{5,4},{6,5},{7,6},{8,15},{9,8},{10,9... | collective-permute-start | bytes 589832 | tf_op jit(solution)/shard_map/while/body/eval_jaxpr/ppermute | solution.py:19
  279.2 12.9 %collective-permute-start.1 = (bf16[128,768]{0,1:T(8,128)(2,1)}, bf16[128,768]{0,1:T(8,128)(2,1)}, u32[]{:S(2)}, u32[]{:S(2)}) collective-permute-start(bf16[128,768]{0,1:T(8,128)(2,1)} %copy.83), channel_id=1, source_target_pairs={{0,7},{1,0},{2,1},{3,2},{4,3},{5,4},{6,5},{7,6},{8,15},{9,8},{10,9... | collective-permute-start | bytes 589832 | tf_op jit(solution)/shard_map/while/body/eval_jaxpr/ppermute | solution.py:19
  293.8 17.3 %collective-permute-start = (bf16[128,768]{0,1:T(8,128)(2,1)}, bf16[128,768]{0,1:T(8,128)(2,1)}, u32[]{:S(2)}, u32[]{:S(2)}) collective-permute-start(bf16[128,768]{0,1:T(8,128)(2,1)} %copy.82), channel_id=1, source_target_pairs={{0,7},{1,0},{2,1},{3,2},{4,3},{5,4},{6,5},{7,6},{8,15},{9,8},{10,9... | collective-permute-start | bytes 589832 | tf_op jit(solution)/shard_map/while/body/eval_jaxpr/ppermute | solution.py:19
  299.1 12.0 %collective-permute-start.1 = (bf16[128,768]{0,1:T(8,128)(2,1)}, bf16[128,768]{0,1:T(8,128)(2,1)}, u32[]{:S(2)}, u32[]{:S(2)}) collective-permute-start(bf16[128,768]{0,1:T(8,128)(2,1)} %copy.83), channel_id=1, source_target_pairs={{0,7},{1,0},{2,1},{3,2},{4,3},{5,4},{6,5},{7,6},{8,15},{9,8},{10,9... | collective-permute-start | bytes 589832 | tf_op jit(solution)/shard_map/while/body/eval_jaxpr/ppermute | solution.py:19
  312.7 17.3 %collective-permute-start = (bf16[128,768]{0,1:T(8,128)(2,1)}, bf16[128,768]{0,1:T(8,128)(2,1)}, u32[]{:S(2)}, u32[]{:S(2)}) collective-permute-start(bf16[128,768]{0,1:T(8,128)(2,1)} %copy.82), channel_id=1, source_target_pairs={{0,7},{1,0},{2,1},{3,2},{4,3},{5,4},{6,5},{7,6},{8,15},{9,8},{10,9... | collective-permute-start | bytes 589832 | tf_op jit(solution)/shard_map/while/body/eval_jaxpr/ppermute | solution.py:19
  331.7 17.3 %collective-permute-start = (bf16[128,768]{0,1:T(8,128)(2,1)}, bf16[128,768]{0,1:T(8,128)(2,1)}, u32[]{:S(2)}, u32[]{:S(2)}) collective-permute-start(bf16[128,768]{0,1:T(8,128)(2,1)} %copy.82), channel_id=1, source_target_pairs={{0,7},{1,0},{2,1},{3,2},{4,3},{5,4},{6,5},{7,6},{8,15},{9,8},{10,9... | collective-permute-start | bytes 589832 | tf_op jit(solution)/shard_map/while/body/eval_jaxpr/ppermute | solution.py:19
  337.0 12.0 %collective-permute-start.1 = (bf16[128,768]{0,1:T(8,128)(2,1)}, bf16[128,768]{0,1:T(8,128)(2,1)}, u32[]{:S(2)}, u32[]{:S(2)}) collective-permute-start(bf16[128,768]{0,1:T(8,128)(2,1)} %copy.83), channel_id=1, source_target_pairs={{0,7},{1,0},{2,1},{3,2},{4,3},{5,4},{6,5},{7,6},{8,15},{9,8},{10,9... | collective-permute-start | bytes 589832 | tf_op jit(solution)/shard_map/while/body/eval_jaxpr/ppermute | solution.py:19
  350.7 17.3 %collective-permute-start = (bf16[128,768]{0,1:T(8,128)(2,1)}, bf16[128,768]{0,1:T(8,128)(2,1)}, u32[]{:S(2)}, u32[]{:S(2)}) collective-permute-start(bf16[128,768]{0,1:T(8,128)(2,1)} %copy.82), channel_id=1, source_target_pairs={{0,7},{1,0},{2,1},{3,2},{4,3},{5,4},{6,5},{7,6},{8,15},{9,8},{10,9... | collective-permute-start | bytes 589832 | tf_op jit(solution)/shard_map/while/body/eval_jaxpr/ppermute | solution.py:19
  369.6 17.3 %collective-permute-start = (bf16[128,768]{0,1:T(8,128)(2,1)}, bf16[128,768]{0,1:T(8,128)(2,1)}, u32[]{:S(2)}, u32[]{:S(2)}) collective-permute-start(bf16[128,768]{0,1:T(8,128)(2,1)} %copy.82), channel_id=1, source_target_pairs={{0,7},{1,0},{2,1},{3,2},{4,3},{5,4},{6,5},{7,6},{8,15},{9,8},{10,9... | collective-permute-start | bytes 589832 | tf_op jit(solution)/shard_map/while/body/eval_jaxpr/ppermute | solution.py:19
  374.9 12.0 %collective-permute-start.1 = (bf16[128,768]{0,1:T(8,128)(2,1)}, bf16[128,768]{0,1:T(8,128)(2,1)}, u32[]{:S(2)}, u32[]{:S(2)}) collective-permute-start(bf16[128,768]{0,1:T(8,128)(2,1)} %copy.83), channel_id=1, source_target_pairs={{0,7},{1,0},{2,1},{3,2},{4,3},{5,4},{6,5},{7,6},{8,15},{9,8},{10,9... | collective-permute-start | bytes 589832 | tf_op jit(solution)/shard_map/while/body/eval_jaxpr/ppermute | solution.py:19
  388.6 17.3 %collective-permute-start = (bf16[128,768]{0,1:T(8,128)(2,1)}, bf16[128,768]{0,1:T(8,128)(2,1)}, u32[]{:S(2)}, u32[]{:S(2)}) collective-permute-start(bf16[128,768]{0,1:T(8,128)(2,1)} %copy.82), channel_id=1, source_target_pairs={{0,7},{1,0},{2,1},{3,2},{4,3},{5,4},{6,5},{7,6},{8,15},{9,8},{10,9... | collective-permute-start | bytes 589832 | tf_op jit(solution)/shard_map/while/body/eval_jaxpr/ppermute | solution.py:19
  393.9 12.0 %collective-permute-start.1 = (bf16[128,768]{0,1:T(8,128)(2,1)}, bf16[128,768]{0,1:T(8,128)(2,1)}, u32[]{:S(2)}, u32[]{:S(2)}) collective-permute-start(bf16[128,768]{0,1:T(8,128)(2,1)} %copy.83), channel_id=1, source_target_pairs={{0,7},{1,0},{2,1},{3,2},{4,3},{5,4},{6,5},{7,6},{8,15},{9,8},{10,9... | collective-permute-start | bytes 589832 | tf_op jit(solution)/shard_map/while/body/eval_jaxpr/ppermute | solution.py:19
  406.6 12.1 %collective-permute-start.5 = (bf16[128,768]{0,1:T(8,128)(2,1)S(1)}, bf16[128,768]{0,1:T(8,128)(2,1)S(1)}, u32[]{:S(2)}, u32[]{:S(2)}) collective-permute-start(bf16[128,768]{0,1:T(8,128)(2,1)S(1)} %add_convert_fusion), channel_id=1, source_target_pairs={{0,7},{1,0},{2,1},{3,2},{4,3},{5,4},{6,5},{7,6},{8,15},{9,8},{10,9... | collective-permute-start | bytes 589832 | tf_op jit(solution)/shard_map/ppermute | solution.py:19
  423.9 107.7 %reduce-scatter.9.cloned.1.call-start = ((), (), s32[]{:S(2)}) async-start(), calls=%async_computation.12 | async-start | bytes 5898240 | tf_op jit(solution)/shard_map/reduce_scatter | solution.py:252
  428.7 162.7 %reduce-scatter.11.cloned.1.call-start = ((), (), s32[]{:S(2)}) async-start(), calls=%async_computation.13 | async-start | bytes 5898240 | tf_op jit(solution)/shard_map/reduce_scatter | solution.py:255
  435.1 244.3 %all-reduce.4.cloned.1.call-start = ((), (), s32[]{:S(2)}) async-start(), calls=%async_computation.14 | async-start | bytes 7077888 | tf_op jit(solution)/shard_map/psum | solution.py:260
  (60 other events, 1217.5 us)
Sparse Core Ops, SparseCore 0:
  9.9 49.8 all-gather.6
  63.3 25.2 all-gather.8
  90.8 24.3 all-gather.10
  116.9 26.7 all-gather.12
  145.4 56.9 all-gather.14
  204.0 56.9 all-gather.16
  273.2 28.6 reduce-scatter.6
  424.0 47.5 reduce-scatter.4
  474.6 56.9 reduce-scatter.8
  534.4 56.9 reduce-scatter.10
  594.1 85.2 all-reduce.3
where the time goes:
time: 694 us; the launch traced here: 693 us
  waiting for transfers between devices  448 us (65%)
  starting transfers between devices  66.9 us (10%)
  local copies, waits for them, and re-layouts  51.3 us (7%)
  matrix products  45.4 us (7%)
  blocking collectives  42 us (6%)
  other arithmetic  22.7 us (3%)
  between operations  14.4 us (2%)
    ppermute x30, starting transfers between devices, from_behind(): return lax.ppermute(value, axis, pairs)  66.2 us
    reduce_scatter x1, waiting for transfers between devices, body(): lax.psum_scatter(local_mats[2].astype(jnp.bfloat16), 'dp', scatter_dimens...  60 us
    reduce_scatter x1, waiting for transfers between devices, body(): lax.psum_scatter(local_mats[3].astype(jnp.bfloat16), 'dp', scatter_dimens...  59.8 us
    all_gather x1, waiting for transfers between devices, body(): lax.all_gather(up_weight, 'dp', axis=0, tiled=True)  56.1 us
    all_gather x1, waiting for transfers between devices, body(): lax.all_gather(down_weight, 'dp', axis=0, tiled=True)  54.3 us
    all_gather x1, waiting for transfers between devices, body(): lax.all_gather(mix_weight, 'dp', axis=0, tiled=True)  49.4 us
    psum x1, blocking collectives, body(): lax.psum((first_gain_grad, first_shift_grad, query_bias_grad, value_bias_...  42 us
    ppermute x30, waiting for transfers between devices, from_behind(): return lax.ppermute(value, axis, pairs)  41.2 us
  transfers between devices with their start and end apart: 41, of which 26 were waited for; matrix products, arithmetic and copies ran while one was open for 13% of the time, Pallas kernels for 0%

commit v1 on v0

--- a/solution.py
+++ b/solution.py
@@ -1,8 +1,11 @@
+import functools
 import math
 
 import jax
 import jax.numpy as jnp
 from jax import lax
+from jax.experimental import pallas as pl
+from jax.experimental.pallas import tpu as pltpu
 from jax.sharding import PartitionSpec as P
 
 H = 12
@@ -295,6 +298,378 @@
     )
 
 
+def flip(index, mask):
+    bit = 1
+    while bit <= mask:
+        if mask & bit:
+            index = index + bit - 2 * bit * ((index // bit) % 2)
+        bit *= 2
+    return index
+
+
+def group_size(group, sizes):
+    return {"dp": sizes[0], "z": sizes[1] // 2, "core": 2}[group]
+
+
+def exchange_kernel(plan, sizes, *refs):
+    count = len(plan)
+    ins, outs = refs[:count], refs[count : 2 * count]
+    send_sem, recv_sem, local_sem = refs[2 * count :]
+    dp, ctx = lax.axis_index("dp"), lax.axis_index("ctx")
+    slots = {"dp": dp, "z": ctx // 2, "core": ctx % 2}
+
+    def peer(group, step):
+        if group == "dp":
+            return (flip(dp, step), ctx)
+        return (dp, flip(ctx, 2 * step if group == "z" else step))
+
+    barrier = pltpu.get_barrier_semaphore()
+    greeted = 0
+    for group in sorted({group for group, mode in plan}):
+        for step in range(1, group_size(group, sizes)):
+            pl.semaphore_signal(
+                barrier, inc=1, device_id=peer(group, step), device_id_type=pl.DeviceIdType.MESH
+            )
+            greeted += 1
+    pl.semaphore_wait(barrier, greeted)
+    copies = []
+    for item, (group, mode) in enumerate(plan):
+        me = slots[group]
+        for step in range(group_size(group, sizes) - 1, 0, -1):
+            source = ins[item].at[flip(me, step)] if mode == "a2a" else ins[item]
+            copy = pltpu.make_async_remote_copy(
+                src_ref=source,
+                dst_ref=outs[item].at[me],
+                send_sem=send_sem.at[item, step],
+                recv_sem=recv_sem.at[item, step],
+                device_id=peer(group, step),
+                device_id_type=pl.DeviceIdType.MESH,
+            )
+            copy.start()
+            copies.append(copy)
+    for item, (group, mode) in enumerate(plan):
+        me = slots[group]
+        source = ins[item].at[me] if mode == "a2a" else ins[item]
+        copy = pltpu.make_async_copy(source, outs[item].at[me], local_sem.at[item])
+        copy.start()
+        copies.append(copy)
+    for copy in copies:
+        copy.wait()
+
+
+def exchange(number, *items):
+    sizes = (lax.axis_size("dp"), lax.axis_size("ctx"))
+    plan = tuple((group, mode) for group, mode, value in items)
+    values = [value for group, mode, value in items]
+    shapes = [
+        jax.ShapeDtypeStruct(
+            value.shape if mode == "a2a" else (group_size(group, sizes),) + value.shape, value.dtype
+        )
+        for group, mode, value in items
+    ]
+    most = max(group_size(group, sizes) for group, mode in plan)
+    return pl.pallas_call(
+        functools.partial(exchange_kernel, plan, sizes),
+        out_shape=shapes,
+        in_specs=[pl.BlockSpec(memory_space=pltpu.VMEM)] * len(values),
+        out_specs=[pl.BlockSpec(memory_space=pl.ANY)] * len(values),
+        scratch_shapes=[
+            pltpu.SemaphoreType.DMA((len(values), most)),
+            pltpu.SemaphoreType.DMA((len(values), most)),
+            pltpu.SemaphoreType.DMA((len(values),)),
+        ],
+        compiler_params=pltpu.CompilerParams(collective_id=number, has_side_effects=True),
+        name="exchange_%d" % number,
+    )(*values)
+
+
+def attend_kernel(scale, q_ref, k_ref, v_ref, qpos_ref, kpos_ref, out_ref, lse_ref):
+    scores = matmul_nt(q_ref[0], k_ref[0]) * scale
+    allowed = kpos_ref[...] <= qpos_ref[...]
+    scores = jnp.where(allowed, scores, -1e30)
+    top = jnp.max(scores, axis=-1, keepdims=True)
+    weights = jnp.exp(scores - top)
+    total = jnp.sum(weights, axis=-1, keepdims=True)
+    mixed = matmul(weights.astype(jnp.bfloat16), v_ref[0])
+    out_ref[0] = (mixed / total).astype(jnp.bfloat16)
+    lse_ref[0] = top + jnp.log(total)
+
+
+def attend_back_kernel(
+    scale, q_ref, k_ref, v_ref, qpos_ref, kpos_ref, out_ref, lse_ref, grad_ref, dq_ref, dk_ref, dv_ref
+):
+    q, k, v, grad = q_ref[0], k_ref[0], v_ref[0], grad_ref[0]
+    delta = jnp.sum(
+        grad.astype(jnp.float32) * out_ref[0].astype(jnp.float32), axis=-1, keepdims=True
+    )
+    scores = matmul_nt(q, k) * scale
+    allowed = kpos_ref[...] <= qpos_ref[...]
+    probs = jnp.where(allowed, jnp.exp(scores - lse_ref[0]), 0.0)
+    dprob = matmul_nt(grad, v)
+    dscore = (probs * (dprob - delta)).astype(jnp.bfloat16)
+    dv_ref[0] = matmul_tn(probs.astype(jnp.bfloat16), grad)
+    dk_ref[0] = matmul_tn(dscore, q) * scale
+    dq_ref[0] = matmul(dscore, k) * scale
+
+
+def per_head(kernel, name, heads, inputs, shared, outs):
+    def whole(shape):
+        return pl.BlockSpec(shape, lambda h: (0,) * len(shape))
+
+    def one(shape):
+        return pl.BlockSpec((1,) + shape[1:], lambda h: (h, 0, 0))
+
+    order = [(value, one(value.shape)) for value in inputs[:3]]
+    order += [(value, whole(value.shape)) for value in shared]
+    order += [(value, one(value.shape)) for value in inputs[3:]]
+    return pl.pallas_call(
+        kernel,
+        grid=(heads,),
+        out_shape=[jax.ShapeDtypeStruct(shape, dtype) for shape, dtype in outs],
+        in_specs=[spec for value, spec in order],
+        out_specs=[one(shape) for shape, dtype in outs],
+        name=name,
+    )(*[value for value, spec in order])
+
+
+def tensor_body(
+    block_input,
+    out_cotangent,
+    first_gain,
+    first_shift,
+    mix_weight,
+    query_bias,
+    value_bias,
+    attn_weight,
+    attn_bias,
+    second_gain,
+    second_shift,
+    up_weight,
+    up_bias,
+    down_weight,
+    down_bias,
+):
+    b16, f32 = jnp.bfloat16, jnp.float32
+    n, nz = lax.axis_size("dp"), lax.axis_size("ctx") // 2
+    rows, width = block_input.shape[1:]
+    total_rows = n * rows
+    shard = width // n
+    heads = H // n
+    hidden = up_weight.shape[1] // n
+    scale = HD ** (-0.5)
+    dp, core = lax.axis_index("dp"), lax.axis_index("ctx") % 2
+    x_rows = block_input.reshape(rows, width)
+    cot = out_cotangent.reshape(rows, width)
+    cot_b = cot.astype(b16)
+
+    def total(value):
+        return jnp.sum(value.astype(f32), axis=0)
+
+    first_hat, first_rstd, first_out = layer_norm(x_rows, first_gain, first_shift)
+    mix_parts = mix_weight.reshape(shard, 3, n, shard).transpose(2, 0, 1, 3).reshape(n, shard, 3 * shard)
+    up_parts = up_weight.reshape(shard, n, hidden).transpose(1, 0, 2)
+    mix_cols, first_all = exchange(
+        0, ("dp", "a2a", mix_parts), ("dp", "ag", first_out.astype(b16))
+    )
+    mix_cols = mix_cols.reshape(width, 3 * shard)
+    first_all = first_all.reshape(total_rows, width)
+    own = lambda vector, size: lax.dynamic_slice(vector, (dp * size,), (size,))
+    mix_bias = jnp.concatenate(
+        [own(query_bias, shard), jnp.zeros((shard,), f32), own(value_bias, shard)]
+    )
+    mixed = (matmul(first_all, mix_cols) + mix_bias).astype(b16)
+    mixed_seq, up_cols, cot_all = exchange(
+        1,
+        ("z", "a2a", mixed.reshape(n, rows, 3 * shard)),
+        ("dp", "a2a", up_parts),
+        ("dp", "ag", cot_b),
+    )
+    up_cols = up_cols.reshape(width, hidden)
+    cot_all = cot_all.reshape(total_rows, width)
+    (kv_seq,) = exchange(2, ("core", "ag", mixed_seq[:, :, shard:]))
+
+    def split_heads(value):
+        return value.reshape(-1, heads, HD).transpose(1, 0, 2)
+
+    def join_heads(value):
+        return value.transpose(1, 0, 2).reshape(-1, shard)
+
+    q_rows, k_rows = nz * rows, 2 * nz * rows
+    kv_flat = kv_seq.reshape(k_rows, 2 * shard)
+    q3 = split_heads(mixed_seq[:, :, :shard])
+    k3, v3 = split_heads(kv_flat[:, :shard]), split_heads(kv_flat[:, shard:])
+    q_idx, k_idx = jnp.arange(q_rows), jnp.arange(k_rows)
+    q_pos = ((q_idx // rows) * 2 + core) * rows + q_idx % rows
+    k_pos = (((k_idx % q_rows) // rows) * 2 + k_idx // q_rows) * rows + k_idx % rows
+    shared = (q_pos.astype(jnp.int32)[:, None], k_pos.astype(jnp.int32)[None, :])
+    out3, lse = per_head(
+        functools.partial(attend_kernel, scale),
+        "attend",
+        heads,
+        (q3, k3, v3),
+        shared,
+        (((heads, q_rows, HD), b16), ((heads, q_rows, 1), f32)),
+    )
+    (attended,) = exchange(3, ("z", "a2a", join_heads(out3).reshape(nz, rows, shard)))
+    attended = attended.reshape(total_rows, shard)
+    (attn_parts,) = exchange(
+        4, ("dp", "a2a", matmul(attended, attn_weight).astype(b16).reshape(n, rows, width))
+    )
+    after_attn = x_rows + total(attn_parts) + attn_bias
+    second_hat, second_rstd, second_out = layer_norm(after_attn, second_gain, second_shift)
+    (second_all,) = exchange(5, ("dp", "ag", second_out.astype(b16)))
+    second_all = second_all.reshape(total_rows, width)
+    pre_act = matmul(second_all, up_cols) + own(up_bias, hidden)
+    act_value, act_slope = gelu_pair(pre_act)
+    activ = act_value.astype(b16)
+    out_part = matmul(activ, down_weight).astype(b16)
+    pre_grad = matmul_nt(cot_all, down_weight) * act_slope
+    pre_grad_b = pre_grad.astype(b16)
+    second_part = matmul_nt(pre_grad_b, up_cols).astype(b16)
+    down_grad = matmul_tn(activ, cot_all).astype(b16)
+    up_grad = matmul_tn(second_all, pre_grad_b).astype(b16)
+    up_bias_grad = jnp.sum(pre_grad, axis=0)
+
+    def halves(value):
+        return value.reshape(value.shape[0], 2, -1).transpose(1, 0, 2)
+
+    out_parts, second_parts, down_pair, up_pair = exchange(
+        6,
+        ("dp", "a2a", out_part.reshape(n, rows, width)),
+        ("dp", "a2a", second_part.reshape(n, rows, width)),
+        ("core", "a2a", halves(down_grad)),
+        ("core", "a2a", halves(up_grad)),
+    )
+    block_output = after_attn + total(out_parts) + down_bias
+    second_grad = total(second_parts)
+    resid_grad = cot + norm_back(second_grad, second_hat, second_rstd, second_gain)
+    down_sum = total(down_pair).astype(b16).reshape(nz, hidden // nz, width // 2)
+
+    def by_rows(value):
+        columns = value.shape[-1]
+        return value.reshape(n, nz, shard // nz, columns).transpose(1, 0, 2, 3)
+
+    up_sum = by_rows(total(up_pair).astype(b16))
+    resid_all, down_z, up_z = exchange(
+        7,
+        ("dp", "ag", resid_grad.astype(b16)),
+        ("z", "a2a", down_sum),
+        ("z", "a2a", up_sum),
+    )
+    resid_all = resid_all.reshape(total_rows, width)
+    attended_grad = matmul_nt(resid_all, attn_weight).astype(b16)
+    attn_grad = matmul_tn(attended, resid_all).astype(b16)
+    down_piece = total(down_z).astype(b16)
+    up_piece = total(up_z).astype(b16)
+    grad_seq, up_dp, attn_pair = exchange(
+        8,
+        ("z", "a2a", attended_grad.reshape(n, rows, shard)),
+        ("dp", "a2a", up_piece),
+        ("core", "a2a", halves(attn_grad)),
+    )
+    dq3, dk3, dv3 = per_head(
+        functools.partial(attend_back_kernel, scale),
+        "attend_back",
+        heads,
+        (q3, k3, v3, out3, lse, split_heads(grad_seq)),
+        shared,
+        (((heads, q_rows, HD), f32), ((heads, k_rows, HD), f32), ((heads, k_rows, HD), f32)),
+    )
+    query_sum = jnp.sum(dq3, axis=1).reshape(shard)
+    value_sum = jnp.sum(dv3, axis=1).reshape(shard)
+    key_value = jnp.concatenate([join_heads(dk3), join_heads(dv3)], axis=1).astype(b16)
+    (kv_pair,) = exchange(9, ("core", "a2a", key_value.reshape(2, nz, rows, 2 * shard)))
+    mixed_back = jnp.concatenate(
+        [join_heads(dq3).astype(b16).reshape(nz, rows, shard), total(kv_pair).astype(b16)], axis=-1
+    )
+    attn_sum = total(attn_pair).astype(b16).reshape(nz, shard // nz, width // 2)
+    mixed_grad, attn_z = exchange(10, ("z", "a2a", mixed_back), ("z", "a2a", attn_sum))
+    mixed_grad = mixed_grad.reshape(total_rows, 3 * shard)
+    first_part = matmul_nt(mixed_grad, mix_cols).astype(b16)
+    mix_grad = matmul_tn(first_all, mixed_grad).astype(b16)
+    attn_piece = total(attn_z).astype(b16)
+    first_parts, mix_pair, down_all, up_all, attn_all = exchange(
+        11,
+        ("dp", "a2a", first_part.reshape(n, rows, width)),
+        ("core", "a2a", halves(mix_grad)),
+        ("z", "ag", down_piece),
+        ("z", "ag", up_dp),
+        ("z", "ag", attn_piece),
+    )
+    first_grad = total(first_parts)
+    input_grad = resid_grad + norm_back(first_grad, first_hat, first_rstd, first_gain)
+
+    def spread(vector, full):
+        return lax.dynamic_update_slice(
+            jnp.zeros((full,), f32), vector, (dp * vector.shape[0],)
+        )
+
+    smalls = [
+        jnp.sum(first_grad * first_hat, axis=0),
+        jnp.sum(first_grad, axis=0),
+        spread(query_sum, width),
+        spread(value_sum, width),
+        jnp.sum(resid_grad, axis=0),
+        jnp.sum(second_grad * second_hat, axis=0),
+        jnp.sum(second_grad, axis=0),
+        spread(up_bias_grad, hidden * n),
+        jnp.sum(cot, axis=0),
+    ]
+    lengths = [vector.shape[0] for vector in smalls]
+    small = jnp.concatenate(smalls).reshape(-1, 128)
+    mix_sum = by_rows(total(mix_pair).astype(b16))
+    mix_z, small_pair, down_full, up_full, attn_full = exchange(
+        12,
+        ("z", "a2a", mix_sum),
+        ("core", "ag", small),
+        ("core", "ag", down_all),
+        ("core", "ag", up_all),
+        ("core", "ag", attn_all),
+    )
+    mix_dp, small_z = exchange(
+        13, ("dp", "a2a", total(mix_z).astype(b16)), ("z", "ag", total(small_pair))
+    )
+    mix_all, small_dp = exchange(14, ("z", "ag", mix_dp), ("dp", "ag", total(small_z)))
+    (mix_full,) = exchange(15, ("core", "ag", mix_all))
+    small = total(small_dp).reshape(-1)
+    vectors, start = [], 0
+    for length in lengths:
+        vectors.append(small[start : start + length])
+        start += length
+    down_out = down_full.transpose(1, 2, 0, 3).reshape(hidden, width).astype(f32)
+    attn_out = attn_full.transpose(1, 2, 0, 3).reshape(shard, width).astype(f32)
+    up_out = up_full.transpose(1, 3, 2, 0, 4).reshape(shard, n * hidden).astype(f32)
+    mix_out = (
+        mix_full.transpose(1, 3, 2, 0, 4)
+        .reshape(shard, n, 3, shard)
+        .transpose(0, 2, 1, 3)
+        .reshape(shard, 3 * width)
+        .astype(f32)
+    )
+    return (
+        block_output.reshape(1, rows, width),
+        input_grad.reshape(1, rows, width),
+        vectors[0],
+        vectors[1],
+        mix_out,
+        vectors[2],
+        vectors[3],
+        attn_out,
+        vectors[4],
+        vectors[5],
+        vectors[6],
+        up_out,
+        vectors[7],
+        down_out,
+        vectors[8],
+    )
+
+
+def fits(mesh):
+    n, ctx = mesh.shape["dp"], mesh.shape["ctx"]
+    return H % n == 0 and ctx == 2 * n and n & (n - 1) == 0
+
+
 def solution(mesh):
     placed = (
         P("dp", "ctx", None),
@@ -314,7 +689,7 @@
         P(),
     )
     return jax.shard_map(
-        body,
+        tensor_body if fits(mesh) else body,
         mesh=mesh,
         in_specs=placed,
         out_specs=(

time: 694 us -> 407 us (0.59)
  waiting for transfers between devices: 448 us -> 0 us
  Pallas kernels: 0 us -> 271 us
  starting transfers between devices: 66.9 us -> 0 us
  blocking collectives: 42 us -> 0 us
  matrix products: 45.4 us -> 23.2 us
  other arithmetic: 22.7 us -> 39.2 us
  local copies, waits for them, and re-layouts: 51.3 us -> 64.3 us
  between operations: 14.4 us -> 1.97 us
    pallas_call x0 -> x18, Pallas kernels: none -> 271 us  [the longest x16 255 us: exchange(): pl.pallas_call(functools.partial(exchange_kernel, plan, sizes), out_shape...]
    all_gather x6 -> x0, waiting for transfers between devices: 210 us -> none  [the longest x1 56.1 us: body(): lax.all_gather(up_weight, 'dp', axis=0, tiled=True)]
    reduce_scatter x4 -> x0, waiting for transfers between devices: 156 us -> none  [the longest x1 60 us: body(): lax.psum_scatter(local_mats[2].astype(jnp.bfloat16), 'dp', scatter_dimens...]
    ppermute x30 -> x0, starting transfers between devices: 66.2 us -> none  [from_behind(): return lax.ppermute(value, axis, pairs)]
    psum x1 -> x0, blocking collectives: 42 us -> none  [body(): lax.psum((first_gain_grad, first_shift_grad, query_bias_grad, value_bias_...]
    ppermute x30 -> x0, waiting for transfers between devices: 41.2 us -> none  [from_behind(): return lax.ppermute(value, axis, pairs)]
    psum x1 -> x0, waiting for transfers between devices: 37.8 us -> none  [body(): lax.psum(shard_sums[0].astype(jnp.bfloat16), 'ctx').astype(jnp.float32)]
    reduce_sum x6 -> x21, other arithmetic: 1.95 us -> 28.6 us  [the longest x13 18.5 us: total(): return jnp.sum(value.astype(f32), axis=0)]
  transfers between devices with their start and end apart: 41 -> 0, of which waited for: 26 -> 0; matrix products, arithmetic and copies ran while one was open for 13% -> 0% of each run, Pallas kernels for 0% -> 0%
where the time goes in v1:
time: 407 us; the launch traced here: 399 us
  Pallas kernels  271 us (67%)
  local copies, waits for them, and re-layouts  64.3 us (16%)
  other arithmetic  39.2 us (10%)
  matrix products  23.2 us (6%)
    pallas_call x16, Pallas kernels, exchange(): pl.pallas_call(functools.partial(exchange_kernel, plan, sizes), out_shape...  255 us
    reduce_sum x13, other arithmetic, total(): return jnp.sum(value.astype(f32), axis=0)  18.5 us
    pallas_call x2, Pallas kernels, per_head(): pl.pallas_call(kernel, grid=(heads,), out_shape=[jax.ShapeDtypeStruct(sha...  15.1 us
    convert_element_type x4, local copies, waits for them, and re-layouts, tensor_body(): mix_out = mix_full.transpose(1, 3, 2, 0, 4).reshape(shard, n, 3, shard).t...  13.8 us
    dot_general x4, matrix products, matmul(): return jnp.dot(a, b, preferred_element_type=jnp.float32)  9.47 us
    dot_general x4, matrix products, matmul_nt(): lax.dot_general(a, b, (((1,), (1,)), ((), ())), preferred_element_type=jn...  8.59 us

profile of v1, /device:TPU:0, one launch (start us, length us, event | category | flops | bytes accessed | tf_op | source)
XLA Modules:
  0.0 399.2 jit_solution(12947651880840207381)
XLA Ops:
  0.7 3.8 reshape.585
  9.5 25.4 %exchange_0.1 = (bf16[4,192,576]{2,1,0:T(8,128)(2,1)}, bf16[4,128,768]{2,1,0:T(8,128)(2,1)}) custom-call(bf16[4,192,576]{2,1,0:T(8,128)(2,1)} %copy.73.refs_0_, bf16[128,768]{1,0:T(8,128)(2,1)} %add_convert_fusion.1.refs_1_), custom_call_target="tpu_custom_call" | custom-call | tf_op jit(solution)/shard_map/exchange_0/pallas_call | solution.py:371
  36.6 3.0 fusion.6
  43.6 27.6 %exchange_1.1 = (bf16[4,128,576]{2,1,0:T(8,128)(2,1)}, bf16[4,192,768]{2,1,0:T(8,128)(2,1)}, bf16[4,128,768]{2,1,0:T(8,128)(2,1)}) custom-call(bf16[4,128,576]{2,1,0:T(8,128)(2,1)} %bitcast.205, bf16[4,192,768]{2,1,0:T(8,128)(2,1)} %bitcast.195, bf16[128,768]{1,0:T(8,128)(2,1)} %get-tuple-element.110.refs_2_), custom_call_target="tpu_custom_call" | custom-call | tf_op jit(solution)/shard_map/exchange_1/pallas_call | solution.py:371
  82.8 6.8 %attend.1 = (bf16[3,512,64]{2,1,0:T(8,128)(2,1)}, f32[3,512,1]{2,1,0:T(8,128)}) custom-call(bf16[3,512,64]{2,1,0:T(8,128)(2,1)} %bitcast.201, bf16[3,1024,64]{2,1,0:T(8,128)(2,1)} %bitcast.191, bf16[3,1024,64]{2,1,0:T(8,128)(2,1)} %bitcast.193, s32[512,1]{1,0:T(8,128)} %fusion.31.qpos_ref, s32[1,1024]{1,0:T(1,128)} %fusion.33.kpos_ref), custom_call_target="tpu_custom_call" | custom-call | tf_op jit(solution)/shard_map/attend/pallas_call | solution.py:425
  91.8 10.4 %exchange_3.1 = bf16[4,128,192]{2,1,0:T(8,128)(2,1)} custom-call(bf16[4,128,192]{2,1,0:T(8,128)(2,1)} %copy.83.refs_0_), custom_call_target="tpu_custom_call" | custom-call | tf_op jit(solution)/shard_map/exchange_3/pallas_call | solution.py:371
  104.4 12.3 %exchange_4.1 = bf16[4,128,768]{2,1,0:T(8,128)(2,1)} custom-call(bf16[4,128,768]{2,1,0:T(8,128)(2,1)} %bitcast.204), custom_call_target="tpu_custom_call" | custom-call | tf_op jit(solution)/shard_map/exchange_4/pallas_call | solution.py:371
  119.2 13.1 %exchange_5.1 = bf16[4,128,768]{2,1,0:T(8,128)(2,1)} custom-call(bf16[128,768]{1,0:T(8,128)(2,1)} %add_convert_fusion.refs_0_), custom_call_target="tpu_custom_call" | custom-call | tf_op jit(solution)/shard_map/exchange_5/pallas_call | solution.py:371
  147.2 22.1 %exchange_6.1 = (bf16[4,128,768]{2,1,0:T(8,128)(2,1)}, bf16[4,128,768]{2,1,0:T(8,128)(2,1)}, bf16[2,768,384]{2,1,0:T(8,128)(2,1)}, bf16[2,768,384]{2,1,0:T(8,128)(2,1)}) custom-call(bf16[4,128,768]{2,1,0:T(8,128)(2,1)} %bitcast.228, bf16[4,128,768]{2,1,0:T(8,128)(2,1)} %bitcast.229, bf16[2,768,384]{2,1,0:T(8,128)(2,1)} %bitcast.198, ...), custom_call_target="tpu_custom_call" | custom-call | tf_op jit(solution)/shard_map/exchange_6/pallas_call | solution.py:371
  179.1 30.2 %exchange_7.1 = (bf16[4,128,768]{2,1,0:T(8,128)(2,1)}, bf16[4,192,384]{2,1,0:T(8,128)(2,1)}, bf16[4,4,48,384]{3,2,1,0:T(8,128)(2,1)}) custom-call(bf16[128,768]{1,0:T(8,128)(2,1)} %get-tuple-element.98.refs_0_, bf16[4,192,384]{2,1,0:T(8,128)(2,1)} %bitcast.212, bf16[4,4,48,384]{3,2,1,0:T(8,128)(2,1)} %bitcast.209), custom_call_target="tpu_custom_call" | custom-call | tf_op jit(solution)/shard_map/exchange_7/pallas_call | solution.py:371
  214.8 9.7 %exchange_8.1 = (bf16[4,128,192]{2,1,0:T(8,128)(2,1)}, bf16[4,48,384]{2,1,0:T(8,128)(2,1)}, bf16[2,192,384]{2,1,0:T(8,128)(2,1)}) custom-call(bf16[4,128,192]{2,1,0:T(8,128)(2,1)} %bitcast.223, bf16[4,48,384]{2,1,0:T(8,128)(2,1)} %reduce_sum.346.refs_1_, bf16[2,192,384]{2,1,0:T(8,128)(2,1)} %bitcast.221), custom_call_target="tpu_custom_call" | custom-call | tf_op jit(solution)/shard_map/exchange_8/pallas_call | solution.py:371
  226.6 8.3 %attend_back.1 = (f32[3,512,64]{2,1,0:T(8,128)}, f32[3,1024,64]{2,1,0:T(8,128)}, f32[3,1024,64]{2,1,0:T(8,128)}) custom-call(bf16[3,512,64]{2,1,0:T(8,128)(2,1)} %bitcast.202, bf16[3,1024,64]{2,1,0:T(8,128)(2,1)} %bitcast.192, bf16[3,1024,64]{2,1,0:T(8,128)(2,1)} %bitcast.194, s32[512,1]{1,0:T(8,128)} %fusion.31.qpos_ref, s32[1,1024]{1,0:T(1,128)} %fusion.33.kpos_ref, ...), custom_call_target="tpu_custom_call" | custom-call | tf_op jit(solution)/shard_map/attend_back/pallas_call | solution.py:425
  243.8 3.1 exchange_9.1
  250.6 22.2 %exchange_10.1 = (bf16[4,128,576]{2,1,0:T(8,128)(2,1)}, bf16[4,48,384]{2,1,0:T(8,128)(2,1)}) custom-call(bf16[4,128,576]{2,1,0:T(8,128)(2,1)} %pad_maximum_fusion.1.refs_0_, bf16[4,48,384]{2,1,0:T(8,128)(2,1)} %bitcast.231), custom_call_target="tpu_custom_call" | custom-call | tf_op jit(solution)/shard_map/exchange_10/pallas_call | solution.py:371
  272.8 3.2 convolution_convert_fusion.4
  281.5 33.4 %exchange_11.1 = (bf16[4,128,768]{2,1,0:T(8,128)(2,1)}, bf16[2,768,288]{2,1,0:T(8,128)(2,1)}, bf16[4,192,384]{2,1,0:T(8,128)(2,1)}, bf16[4,4,48,384]{3,2,1,0:T(8,128)(2,1)}, bf16[4,48,384]{2,1,0:T(8,128)(2,1)}) custom-call(bf16[4,128,768]{2,1,0:T(8,128)(2,1)} %bitcast.225, bf16[2,768,288]{2,1,0:T(8,128)(2,1)} %bitcast.197, ...), custom_call_target="tpu_custom_call" | custom-call | tf_op jit(solution)/shard_map/exchange_11/pallas_call | solution.py:371
  322.4 17.2 %exchange_12.1 = (bf16[4,4,48,288]{3,2,1,0:T(8,128)(2,1)}, f32[2,72,128]{2,1,0:T(8,128)}, bf16[2,4,192,384]{3,2,1,0:T(8,128)(2,1)}, bf16[2,4,4,48,384]{4,3,2,1,0:T(8,128)(2,1)}, bf16[2,4,48,384]{3,2,1,0:T(8,128)(2,1)}) custom-call(bf16[4,4,48,288]{3,2,1,0:T(8,128)(2,1)} %bitcast.208, f32[72,128]{1,0:T(8,128)} %bitcast.232, ...), custom_call_target="tpu_custom_call" | custom-call | tf_op jit(solution)/shard_map/exchange_12/pallas_call | solution.py:371
  343.1 6.9 %exchange_13.1 = (bf16[4,48,288]{2,1,0:T(8,128)(2,1)}, f32[4,72,128]{2,1,0:T(8,128)}) custom-call(bf16[4,48,288]{2,1,0:T(8,128)(2,1)} %reduce_sum.365.refs_0_, f32[72,128]{1,0:T(8,128)} %reduce_sum.366.refs_1_), custom_call_target="tpu_custom_call" | custom-call | tf_op jit(solution)/shard_map/exchange_13/pallas_call | solution.py:371
  351.6 15.7 %exchange_14.1 = (bf16[4,4,48,288]{3,2,1,0:T(8,128)(2,1)}, f32[4,72,128]{2,1,0:T(8,128)}) custom-call(bf16[4,48,288]{2,1,0:T(8,128)(2,1)} %get-tuple-element.80.refs_0_, f32[72,128]{1,0:T(8,128)} %reduce_sum.367.refs_1_), custom_call_target="tpu_custom_call" | custom-call | tf_op jit(solution)/shard_map/exchange_14/pallas_call | solution.py:371
  368.9 3.2 exchange_15.1
  373.6 3.2 copy.101
  376.8 4.8 %reshape.624 = f32[192,4,3,192]{3,2,1,0:T(4,128)S(1)} reshape(f32[4,48,4,2,288]{4,3,2,1,0:T(2,128)} %copy.101) | data formatting | bytes 3538944 | tf_op jit(solution)/shard_map/convert_element_type | solution.py:647
  383.7 3.7 reshape.620
  390.8 2.9 reshape.622
  (217 shorter events, 104.8 us)
Async XLA Ops:
  0.6 134.7 %copy-start = (bf16[768,768]{1,0:T(8,128)(2,1)S(1)}, bf16[768,768]{1,0:T(8,128)(2,1)}, u32[]{:S(2)}) copy-start(bf16[768,768]{1,0:T(8,128)(2,1)} %param.28) | copy-start | bytes 3538948
  8.5 31.1 %copy-start.27 = (f32[128]{0:T(128)}, f32[128]{0:T(128)S(1)}, u32[]{:S(2)}) copy-start(f32[128]{0:T(128)S(1)} %broadcast_multiply_fusion.5) | copy-start | bytes 1540
  8.7 30.9 %copy-start.32 = (f32[128]{0:T(128)}, f32[128]{0:T(128)S(1)}, u32[]{:S(2)}) copy-start(f32[128]{0:T(128)S(1)} %add_rsqrt_fusion.1) | copy-start | bytes 1540
  36.6 5.2 %copy-start.9 = (bf16[192,3072]{1,0:T(8,128)(2,1)S(1)}, bf16[192,3072]{1,0:T(8,128)(2,1)}, u32[]{:S(2)}) copy-start(bf16[192,3072]{1,0:T(8,128)(2,1)} %param.26) | copy-start | bytes 3538948
  82.8 19.4 %copy-start.10 = (bf16[192,768]{1,0:T(8,128)(2,1)S(1)}, bf16[192,768]{1,0:T(8,128)(2,1)}, u32[]{:S(2)}) copy-start(bf16[192,768]{1,0:T(8,128)(2,1)} %param.22) | copy-start | bytes 884740
  104.4 13.6 %copy-start.21 = (f32[768]{0:T(1024)S(1)}, f32[768]{0:T(1024)}, u32[]{:S(2)}) copy-start(f32[768]{0:T(1024)} %param.23) | copy-start | bytes 9220
  118.2 54.4 %copy-start.25 = (f32[128]{0:T(128)}, f32[128]{0:T(128)S(1)}, u32[]{:S(2)}) copy-start(f32[128]{0:T(128)S(1)} %broadcast_multiply_fusion.4) | copy-start | bytes 1540
  118.4 54.1 %copy-start.29 = (f32[128]{0:T(128)}, f32[128]{0:T(128)S(1)}, u32[]{:S(2)}) copy-start(f32[128]{0:T(128)S(1)} %add_rsqrt_fusion) | copy-start | bytes 1540
  172.5 3.9 copy-start.38
  172.6 3.9 copy-start.40
  209.3 4.3 %copy-start.4 = (bf16[4,128,768]{2,1,0:T(8,128)(2,1)S(1)}, bf16[4,128,768]{2,1,0:T(8,128)(2,1)}, u32[]{:S(2)}) copy-start(bf16[4,128,768]{2,1,0:T(8,128)(2,1)} %get-tuple-element.62) | copy-start | bytes 2359300
  209.3 4.3 %copy-start.5 = (bf16[4,128,192]{2,1,0:T(8,128)(2,1)S(1)}, bf16[4,128,192]{2,1,0:T(8,128)(2,1)}, u32[]{:S(2)}) copy-start(bf16[4,128,192]{2,1,0:T(8,128)(2,1)} %exchange_3.1) | copy-start | bytes 589828
  243.8 4.4 %copy-start.11 = (f32[3,512,64]{2,1,0:T(8,128)S(1)}, f32[3,512,64]{2,1,0:T(8,128)}, u32[]{:S(2)}) copy-start(f32[3,512,64]{2,1,0:T(8,128)} %get-tuple-element.65) | copy-start | bytes 1179652
  281.4 34.9 %copy-start.28 = (f32[128]{0:T(128)S(1)}, f32[128]{0:T(128)}, u32[]{:S(2)}) copy-start(f32[128]{0:T(128)} %copy-done.27) | copy-start | bytes 1540
  281.4 34.9 %copy-start.33 = (f32[128]{0:T(128)S(1)}, f32[128]{0:T(128)}, u32[]{:S(2)}) copy-start(f32[128]{0:T(128)} %copy-done.32) | copy-start | bytes 1540
  281.5 35.2 %copy-start.6 = (f32[128,768]{1,0:T(8,128)S(1)}, f32[128,768]{1,0:T(8,128)}, u32[]{:S(2)}) copy-start(f32[128,768]{1,0:T(8,128)} %get-tuple-element.121) | copy-start | bytes 1179652
  281.5 35.2 %copy-start.26 = (f32[128]{0:T(128)S(1)}, f32[128]{0:T(128)}, u32[]{:S(2)}) copy-start(f32[128]{0:T(128)} %copy-done.25) | copy-start | bytes 1540
  281.5 35.2 %copy-start.30 = (f32[128]{0:T(128)S(1)}, f32[128]{0:T(128)}, u32[]{:S(2)}) copy-start(f32[128]{0:T(128)} %copy-done.29) | copy-start | bytes 1540
  281.5 35.2 %copy-start.36 = (f32[768]{0:T(1024)S(1)}, f32[768]{0:T(1024)}, u32[]{:S(2)}) copy-start(f32[768]{0:T(1024)} %param.29) | copy-start | bytes 9220
  281.5 35.2 %copy-start.39 = (f32[128]{0:T(128)S(1)}, f32[128]{0:T(128)}, u32[]{:S(2)}) copy-start(f32[128]{0:T(128)} %copy-done.38) | copy-start | bytes 1540
  281.5 35.2 %copy-start.41 = (f32[128]{0:T(128)S(1)}, f32[128]{0:T(128)}, u32[]{:S(2)}) copy-start(f32[128]{0:T(128)} %copy-done.40) | copy-start | bytes 1540
  368.2 5.4 %copy-start.16 = (f32[72,128]{1,0:T(8,128)}, f32[72,128]{1,0:T(8,128)S(1)}, u32[]{:S(2)}) copy-start(f32[72,128]{1,0:T(8,128)S(1)} %reduce_sum.368) | copy-start | bytes 110596
  383.7 3.7 copy-start.14
  390.8 4.3 %copy-start.7 = (bf16[2,4,192,384]{3,2,1,0:T(8,128)(2,1)S(1)}, bf16[2,4,192,384]{3,2,1,0:T(8,128)(2,1)}, u32[]{:S(2)}) copy-start(bf16[2,4,192,384]{3,2,1,0:T(8,128)(2,1)} %get-tuple-element.86) | copy-start | bytes 3538948
  (23 other events, 53.2 us)

commit v2 on v1

--- a/solution.py
+++ b/solution.py
@@ -335,26 +335,57 @@
     copies = []
     for item, (group, mode) in enumerate(plan):
         me = slots[group]
-        for step in range(group_size(group, sizes) - 1, 0, -1):
-            source = ins[item].at[flip(me, step)] if mode == "a2a" else ins[item]
-            copy = pltpu.make_async_remote_copy(
-                src_ref=source,
-                dst_ref=outs[item].at[me],
-                send_sem=send_sem.at[item, step],
-                recv_sem=recv_sem.at[item, step],
-                device_id=peer(group, step),
-                device_id_type=pl.DeviceIdType.MESH,
-            )
-            copy.start()
-            copies.append(copy)
-    for item, (group, mode) in enumerate(plan):
-        me = slots[group]
-        source = ins[item].at[me] if mode == "a2a" else ins[item]
-        copy = pltpu.make_async_copy(source, outs[item].at[me], local_sem.at[item])
-        copy.start()
-        copies.append(copy)
+        for step in range(group_size(group, sizes) - 1, -1, -1):
+            pieces = piece_refs(ins[item], outs[item], mode, me, flip(me, step))
+            for part, (source, target) in enumerate(pieces):
+                number = step * PARTS + part
+                if step == 0:
+                    copy = pltpu.make_async_copy(source, target, local_sem.at[item, part])
+                else:
+                    copy = pltpu.make_async_remote_copy(
+                        src_ref=source,
+                        dst_ref=target,
+                        send_sem=send_sem.at[item, number],
+                        recv_sem=recv_sem.at[item, number],
+                        device_id=peer(group, step),
+                        device_id_type=pl.DeviceIdType.MESH,
+                    )
+                copy.start()
+                copies.append(copy)
     for copy in copies:
         copy.wait()
+
+
+PARTS = 4
+
+
+def piece_refs(source, target, mode, me, other):
+    if mode == "a2a":
+        return [(source.at[other], target.at[me])]
+    if mode == "cols":
+        size = target.shape[2]
+        return [(source.at[:, pl.ds(pl.multiple_of(other * size, 128), size)], target.at[me])]
+    if mode == "lanes":
+        parts, size = source.shape[1], source.shape[3]
+        step = target.shape[2] // parts
+        return [
+            (
+                source.at[:, part],
+                target.at[:, :, pl.ds(pl.multiple_of(part * step + me * size, 128), size)],
+            )
+            for part in range(parts)
+        ]
+    return [(source, target.at[me])]
+
+
+def exchange_shape(shape, mode, n):
+    if mode == "a2a":
+        return shape
+    if mode == "cols":
+        return (n, shape[0], shape[1] // n)
+    if mode == "lanes":
+        return (shape[0], shape[2], shape[1] * n * shape[3])
+    return (n,) + shape
 
 
 def exchange(number, *items):
@@ -363,11 +394,11 @@
     values = [value for group, mode, value in items]
     shapes = [
         jax.ShapeDtypeStruct(
-            value.shape if mode == "a2a" else (group_size(group, sizes),) + value.shape, value.dtype
+            exchange_shape(value.shape, mode, group_size(group, sizes)), value.dtype
         )
         for group, mode, value in items
     ]
-    most = max(group_size(group, sizes) for group, mode in plan)
+    most = PARTS * max(group_size(group, sizes) for group, mode in plan)
     return pl.pallas_call(
         functools.partial(exchange_kernel, plan, sizes),
         out_shape=shapes,
@@ -376,60 +407,69 @@
         scratch_shapes=[
             pltpu.SemaphoreType.DMA((len(values), most)),
             pltpu.SemaphoreType.DMA((len(values), most)),
-            pltpu.SemaphoreType.DMA((len(values),)),
+            pltpu.SemaphoreType.DMA((len(values), PARTS)),
         ],
         compiler_params=pltpu.CompilerParams(collective_id=number, has_side_effects=True),
         name="exchange_%d" % number,
     )(*values)
 
 
-def attend_kernel(scale, q_ref, k_ref, v_ref, qpos_ref, kpos_ref, out_ref, lse_ref):
-    scores = matmul_nt(q_ref[0], k_ref[0]) * scale
+def head_columns(ref, part, head, heads):
+    start = (part * heads + head) * HD
+    return ref[:, start : start + HD]
+
+
+def attend_kernel(scale, heads, mixed_ref, kv_ref, qpos_ref, kpos_ref, out_ref, lse_ref):
     allowed = kpos_ref[...] <= qpos_ref[...]
-    scores = jnp.where(allowed, scores, -1e30)
-    top = jnp.max(scores, axis=-1, keepdims=True)
-    weights = jnp.exp(scores - top)
-    total = jnp.sum(weights, axis=-1, keepdims=True)
-    mixed = matmul(weights.astype(jnp.bfloat16), v_ref[0])
-    out_ref[0] = (mixed / total).astype(jnp.bfloat16)
-    lse_ref[0] = top + jnp.log(total)
+    for head in range(heads):
+        q = head_columns(mixed_ref, 0, head, heads)
+        k = head_columns(kv_ref, 0, head, heads)
+        v = head_columns(kv_ref, 1, head, heads)
+        scores = jnp.where(allowed, matmul_nt(q, k) * scale, -1e30)
+        top = jnp.max(scores, axis=-1, keepdims=True)
+        weights = jnp.exp(scores - top)
+        total = jnp.sum(weights, axis=-1, keepdims=True)
+        result = matmul(weights.astype(jnp.bfloat16), v) / total
+        out_ref[:, head * HD : (head + 1) * HD] = result.astype(jnp.bfloat16)
+        lse_ref[:, head : head + 1] = top + jnp.log(total)
 
 
 def attend_back_kernel(
-    scale, q_ref, k_ref, v_ref, qpos_ref, kpos_ref, out_ref, lse_ref, grad_ref, dq_ref, dk_ref, dv_ref
+    scale, heads, mixed_ref, kv_ref, qpos_ref, kpos_ref, out_ref, lse_ref, grad_ref,
+    dq_ref, dkv_ref, qsum_ref, vsum_ref,
 ):
-    q, k, v, grad = q_ref[0], k_ref[0], v_ref[0], grad_ref[0]
-    delta = jnp.sum(
-        grad.astype(jnp.float32) * out_ref[0].astype(jnp.float32), axis=-1, keepdims=True
-    )
-    scores = matmul_nt(q, k) * scale
     allowed = kpos_ref[...] <= qpos_ref[...]
-    probs = jnp.where(allowed, jnp.exp(scores - lse_ref[0]), 0.0)
-    dprob = matmul_nt(grad, v)
-    dscore = (probs * (dprob - delta)).astype(jnp.bfloat16)
-    dv_ref[0] = matmul_tn(probs.astype(jnp.bfloat16), grad)
-    dk_ref[0] = matmul_tn(dscore, q) * scale
-    dq_ref[0] = matmul(dscore, k) * scale
-
-
-def per_head(kernel, name, heads, inputs, shared, outs):
-    def whole(shape):
-        return pl.BlockSpec(shape, lambda h: (0,) * len(shape))
-
-    def one(shape):
-        return pl.BlockSpec((1,) + shape[1:], lambda h: (h, 0, 0))
-
-    order = [(value, one(value.shape)) for value in inputs[:3]]
-    order += [(value, whole(value.shape)) for value in shared]
-    order += [(value, one(value.shape)) for value in inputs[3:]]
+    for head in range(heads):
+        q = head_columns(mixed_ref, 0, head, heads)
+        k = head_columns(kv_ref, 0, head, heads)
+        v = head_columns(kv_ref, 1, head, heads)
+        grad = head_columns(grad_ref, 0, head, heads)
+        out = head_columns(out_ref, 0, head, heads)
+        delta = jnp.sum(
+            grad.astype(jnp.float32) * out.astype(jnp.float32), axis=-1, keepdims=True
+        )
+        lse = lse_ref[:, head : head + 1]
+        probs = jnp.where(allowed, jnp.exp(matmul_nt(q, k) * scale - lse), 0.0)
+        dscore = (probs * (matmul_nt(grad, v) - delta)).astype(jnp.bfloat16)
+        dv = matmul_tn(probs.astype(jnp.bfloat16), grad)
+        dk = matmul_tn(dscore, q) * scale
+        dq = matmul(dscore, k) * scale
+        first, last = head * HD, (head + 1) * HD
+        dq_ref[:, first:last] = dq.astype(jnp.bfloat16)
+        dkv_ref[:, first:last] = dk.astype(jnp.bfloat16)
+        dkv_ref[:, heads * HD + first : heads * HD + last] = dv.astype(jnp.bfloat16)
+        qsum_ref[:, first:last] = jnp.sum(dq, axis=0, keepdims=True)
+        vsum_ref[:, first:last] = jnp.sum(dv, axis=0, keepdims=True)
+
+
+def local_call(kernel, name, values, outs):
     return pl.pallas_call(
         kernel,
-        grid=(heads,),
         out_shape=[jax.ShapeDtypeStruct(shape, dtype) for shape, dtype in outs],
-        in_specs=[spec for value, spec in order],
-        out_specs=[one(shape) for shape, dtype in outs],
+        in_specs=[pl.BlockSpec(memory_space=pltpu.VMEM)] * len(values),
+        out_specs=[pl.BlockSpec(memory_space=pltpu.VMEM)] * len(outs),
         name=name,
-    )(*[value for value, spec in order])
+    )(*values)
 
 
 def tensor_body(
@@ -467,7 +507,6 @@
 
     first_hat, first_rstd, first_out = layer_norm(x_rows, first_gain, first_shift)
     mix_parts = mix_weight.reshape(shard, 3, n, shard).transpose(2, 0, 1, 3).reshape(n, shard, 3 * shard)
-    up_parts = up_weight.reshape(shard, n, hidden).transpose(1, 0, 2)
     mix_cols, first_all = exchange(
         0, ("dp", "a2a", mix_parts), ("dp", "ag", first_out.astype(b16))
     )
@@ -478,39 +517,29 @@
         [own(query_bias, shard), jnp.zeros((shard,), f32), own(value_bias, shard)]
     )
     mixed = (matmul(first_all, mix_cols) + mix_bias).astype(b16)
-    mixed_seq, up_cols, cot_all = exchange(
-        1,
-        ("z", "a2a", mixed.reshape(n, rows, 3 * shard)),
-        ("dp", "a2a", up_parts),
-        ("dp", "ag", cot_b),
+    mixed_seq, up_cols = exchange(
+        1, ("z", "a2a", mixed.reshape(n, rows, 3 * shard)), ("dp", "cols", up_weight)
     )
     up_cols = up_cols.reshape(width, hidden)
-    cot_all = cot_all.reshape(total_rows, width)
     (kv_seq,) = exchange(2, ("core", "ag", mixed_seq[:, :, shard:]))
-
-    def split_heads(value):
-        return value.reshape(-1, heads, HD).transpose(1, 0, 2)
-
-    def join_heads(value):
-        return value.transpose(1, 0, 2).reshape(-1, shard)
 
     q_rows, k_rows = nz * rows, 2 * nz * rows
     kv_flat = kv_seq.reshape(k_rows, 2 * shard)
-    q3 = split_heads(mixed_seq[:, :, :shard])
-    k3, v3 = split_heads(kv_flat[:, :shard]), split_heads(kv_flat[:, shard:])
+    mixed_flat = mixed_seq.reshape(q_rows, 3 * shard)
     q_idx, k_idx = jnp.arange(q_rows), jnp.arange(k_rows)
     q_pos = ((q_idx // rows) * 2 + core) * rows + q_idx % rows
     k_pos = (((k_idx % q_rows) // rows) * 2 + k_idx // q_rows) * rows + k_idx % rows
     shared = (q_pos.astype(jnp.int32)[:, None], k_pos.astype(jnp.int32)[None, :])
-    out3, lse = per_head(
-        functools.partial(attend_kernel, scale),
+    out_seq, lse = local_call(
+        functools.partial(attend_kernel, scale, heads),
         "attend",
-        heads,
-        (q3, k3, v3),
-        shared,
-        (((heads, q_rows, HD), b16), ((heads, q_rows, 1), f32)),
-    )
-    (attended,) = exchange(3, ("z", "a2a", join_heads(out3).reshape(nz, rows, shard)))
+        (mixed_flat, kv_flat) + shared,
+        (((q_rows, shard), b16), ((q_rows, heads), f32)),
+    )
+    attended, cot_all = exchange(
+        3, ("z", "a2a", out_seq.reshape(nz, rows, shard)), ("dp", "ag", cot_b)
+    )
+    cot_all = cot_all.reshape(total_rows, width)
     attended = attended.reshape(total_rows, shard)
     (attn_parts,) = exchange(
         4, ("dp", "a2a", matmul(attended, attn_weight).astype(b16).reshape(n, rows, width))
@@ -533,27 +562,25 @@
     def halves(value):
         return value.reshape(value.shape[0], 2, -1).transpose(1, 0, 2)
 
-    out_parts, second_parts, down_pair, up_pair = exchange(
+    def by_rows(value):
+        columns = value.shape[-1]
+        return value.reshape(n, nz, shard // nz, columns).transpose(1, 0, 2, 3)
+
+    down_pair, up_pair = exchange(16, ("core", "cols", down_grad), ("core", "cols", up_grad))
+    down_sum = total(down_pair).astype(b16).reshape(nz, hidden // nz, width // 2)
+    up_sum = by_rows(total(up_pair).astype(b16))
+    out_parts, second_parts, down_z = exchange(
         6,
         ("dp", "a2a", out_part.reshape(n, rows, width)),
         ("dp", "a2a", second_part.reshape(n, rows, width)),
-        ("core", "a2a", halves(down_grad)),
-        ("core", "a2a", halves(up_grad)),
+        ("z", "a2a", down_sum),
     )
     block_output = after_attn + total(out_parts) + down_bias
     second_grad = total(second_parts)
     resid_grad = cot + norm_back(second_grad, second_hat, second_rstd, second_gain)
-    down_sum = total(down_pair).astype(b16).reshape(nz, hidden // nz, width // 2)
-
-    def by_rows(value):
-        columns = value.shape[-1]
-        return value.reshape(n, nz, shard // nz, columns).transpose(1, 0, 2, 3)
-
-    up_sum = by_rows(total(up_pair).astype(b16))
-    resid_all, down_z, up_z = exchange(
+    resid_all, up_z = exchange(
         7,
         ("dp", "ag", resid_grad.astype(b16)),
-        ("z", "a2a", down_sum),
         ("z", "a2a", up_sum),
     )
     resid_all = resid_all.reshape(total_rows, width)
@@ -565,22 +592,23 @@
         8,
         ("z", "a2a", attended_grad.reshape(n, rows, shard)),
         ("dp", "a2a", up_piece),
-        ("core", "a2a", halves(attn_grad)),
-    )
-    dq3, dk3, dv3 = per_head(
-        functools.partial(attend_back_kernel, scale),
+        ("core", "cols", attn_grad),
+    )
+    query_grad, key_value, query_sum, value_sum = local_call(
+        functools.partial(attend_back_kernel, scale, heads),
         "attend_back",
-        heads,
-        (q3, k3, v3, out3, lse, split_heads(grad_seq)),
-        shared,
-        (((heads, q_rows, HD), f32), ((heads, k_rows, HD), f32), ((heads, k_rows, HD), f32)),
-    )
-    query_sum = jnp.sum(dq3, axis=1).reshape(shard)
-    value_sum = jnp.sum(dv3, axis=1).reshape(shard)
-    key_value = jnp.concatenate([join_heads(dk3), join_heads(dv3)], axis=1).astype(b16)
+        (mixed_flat, kv_flat) + shared + (out_seq, lse, grad_seq.reshape(q_rows, shard)),
+        (
+            ((q_rows, shard), b16),
+            ((k_rows, 2 * shard), b16),
+            ((1, shard), f32),
+            ((1, shard), f32),
+        ),
+    )
+    query_sum, value_sum = query_sum.reshape(shard), value_sum.reshape(shard)
     (kv_pair,) = exchange(9, ("core", "a2a", key_value.reshape(2, nz, rows, 2 * shard)))
     mixed_back = jnp.concatenate(
-        [join_heads(dq3).astype(b16).reshape(nz, rows, shard), total(kv_pair).astype(b16)], axis=-1
+        [query_grad.reshape(nz, rows, shard), total(kv_pair).astype(b16)], axis=-1
     )
     attn_sum = total(attn_pair).astype(b16).reshape(nz, shard // nz, width // 2)
     mixed_grad, attn_z = exchange(10, ("z", "a2a", mixed_back), ("z", "a2a", attn_sum))
@@ -588,11 +616,10 @@
     first_part = matmul_nt(mixed_grad, mix_cols).astype(b16)
     mix_grad = matmul_tn(first_all, mixed_grad).astype(b16)
     attn_piece = total(attn_z).astype(b16)
-    first_parts, mix_pair, down_all, up_all, attn_all = exchange(
+    first_parts, mix_pair, up_all, attn_all = exchange(
         11,
         ("dp", "a2a", first_part.reshape(n, rows, width)),
         ("core", "a2a", halves(mix_grad)),
-        ("z", "ag", down_piece),
         ("z", "ag", up_dp),
         ("z", "ag", attn_piece),
     )
@@ -618,27 +645,34 @@
     lengths = [vector.shape[0] for vector in smalls]
     small = jnp.concatenate(smalls).reshape(-1, 128)
     mix_sum = by_rows(total(mix_pair).astype(b16))
-    mix_z, small_pair, down_full, up_full, attn_full = exchange(
+    mix_z, small_pair, up_full, attn_full = exchange(
         12,
         ("z", "a2a", mix_sum),
         ("core", "ag", small),
-        ("core", "ag", down_all),
-        ("core", "ag", up_all),
-        ("core", "ag", attn_all),
-    )
-    mix_dp, small_z = exchange(
-        13, ("dp", "a2a", total(mix_z).astype(b16)), ("z", "ag", total(small_pair))
-    )
-    mix_all, small_dp = exchange(14, ("z", "ag", mix_dp), ("dp", "ag", total(small_z)))
+        ("core", "lanes", up_all),
+        ("core", "lanes", attn_all[:, None]),
+    )
+    mix_dp, small_z, down_all = exchange(
+        13,
+        ("dp", "a2a", total(mix_z).astype(b16)),
+        ("z", "ag", total(small_pair)),
+        ("z", "ag", down_piece),
+    )
+    mix_all, small_dp, down_full = exchange(
+        14,
+        ("z", "ag", mix_dp),
+        ("dp", "ag", total(small_z)),
+        ("core", "lanes", down_all[:, None]),
+    )
     (mix_full,) = exchange(15, ("core", "ag", mix_all))
     small = total(small_dp).reshape(-1)
     vectors, start = [], 0
     for length in lengths:
         vectors.append(small[start : start + length])
         start += length
-    down_out = down_full.transpose(1, 2, 0, 3).reshape(hidden, width).astype(f32)
-    attn_out = attn_full.transpose(1, 2, 0, 3).reshape(shard, width).astype(f32)
-    up_out = up_full.transpose(1, 3, 2, 0, 4).reshape(shard, n * hidden).astype(f32)
+    down_out = down_full.reshape(hidden, width).astype(f32)
+    attn_out = attn_full.reshape(shard, width).astype(f32)
+    up_out = up_full.reshape(shard, n * hidden).astype(f32)
     mix_out = (
         mix_full.transpose(1, 3, 2, 0, 4)
         .reshape(shard, n, 3, shard)
@@ -667,7 +701,7 @@
 
 def fits(mesh):
     n, ctx = mesh.shape["dp"], mesh.shape["ctx"]
-    return H % n == 0 and ctx == 2 * n and n & (n - 1) == 0
+    return H % n == 0 and ctx == 2 * n and n == PARTS
 
 
 def solution(mesh):

time: 407 us -> 366 us (0.90); the launches traced: 399 us -> 362 us
  local copies, waits for them, and re-layouts: 64.3 us -> 35.9 us
  Pallas kernels: 271 us -> 266 us
    convert_element_type x7 -> x0, local copies, waits for them, and re-layouts: 7.41 us -> none  [the longest x2 4.76 us: tensor_body(): up_full.transpose(1, 3, 2, 0, 4).reshape(shard, n * hidden).astype(f32)]
    reshape x9 -> x0, local copies, waits for them, and re-layouts: 5.58 us -> none  [the longest x6 4.33 us: split_heads(): return value.reshape(-1, heads, HD).transpose(1, 0, 2)]
    pallas_call x16 -> x17, Pallas kernels: 255 us -> 252 us  [exchange(): pl.pallas_call(functools.partial(exchange_kernel, plan, sizes), out_shape...]
where the time goes in v2:
time: 366 us; the launch traced here: 362 us
  Pallas kernels  266 us (73%)
  local copies, waits for them, and re-layouts  35.9 us (10%)
  other arithmetic  35.6 us (10%)
  matrix products  23.6 us (6%)
    pallas_call x17, Pallas kernels, exchange(): pl.pallas_call(functools.partial(exchange_kernel, plan, sizes), out_shape...  252 us
    reduce_sum x13, other arithmetic, total(): return jnp.sum(value.astype(f32), axis=0)  18.5 us
    convert_element_type x4, local copies, waits for them, and re-layouts, tensor_body(): mix_out = mix_full.transpose(1, 3, 2, 0, 4).reshape(shard, n, 3, shard).t...  13.8 us
    pallas_call x2, Pallas kernels, local_call(): pl.pallas_call(kernel, out_shape=[jax.ShapeDtypeStruct(shape, dtype) for...  13.3 us
    dot_general x4, matrix products, matmul_nt(): lax.dot_general(a, b, (((1,), (1,)), ((), ())), preferred_element_type=jn...  8.65 us
    dot_general x4, matrix products, matmul(): return jnp.dot(a, b, preferred_element_type=jnp.float32)  8.55 us
    reshape x3, local copies, waits for them, and re-layouts, tensor_body(): mix_weight.reshape(shard, 3, n, shard).transpose(2, 0, 1, 3)  7.77 us

profile of v2, /device:TPU:0, one launch (start us, length us, event | category | flops | bytes accessed | tf_op | source)
XLA Modules:
  0.0 362.5 jit_solution(317708670289582525)
XLA Ops:
  0.7 3.8 %reshape.563 = bf16[192,3,4,192]{3,2,1,0:T(4,128)(2,1)} reshape(bf16[192,2304]{1,0:T(8,128)(2,1)} %param.19) | data formatting | bytes 1769472 | tf_op jit(solution)/shard_map/reshape | solution.py:509
  9.7 25.9 %exchange_0.1 = (bf16[4,192,576]{2,1,0:T(8,128)(2,1)}, bf16[4,128,768]{2,1,0:T(8,128)(2,1)}) custom-call(bf16[4,192,576]{2,1,0:T(8,128)(2,1)} %copy.46.refs_0_, bf16[128,768]{1,0:T(8,128)(2,1)} %add_convert_fusion.1.refs_1_), custom_call_target="tpu_custom_call" | custom-call | tf_op jit(solution)/shard_map/exchange_0/pallas_call | solution.py:402
  40.4 20.9 %exchange_1.1 = (bf16[4,128,576]{2,1,0:T(8,128)(2,1)}, bf16[4,192,768]{2,1,0:T(8,128)(2,1)}) custom-call(bf16[4,128,576]{2,1,0:T(8,128)(2,1)} %bitcast.161, bf16[192,3072]{1,0:T(8,128)(2,1)} %refs_1_.1), custom_call_target="tpu_custom_call" | custom-call | tf_op jit(solution)/shard_map/exchange_1/pallas_call | solution.py:402
  63.3 3.1 exchange_2.1
  67.8 5.5 %attend.1 = (bf16[512,192]{1,0:T(8,128)(2,1)}, f32[512,3]{1,0:T(8,128)}) custom-call(bf16[512,576]{1,0:T(8,128)(2,1)} %bitcast.157, bf16[1024,384]{1,0:T(8,128)(2,1)} %bitcast.153, s32[512,1]{1,0:T(8,128)} %fusion.31.qpos_ref, s32[1,1024]{1,0:T(1,128)} %fusion.33.kpos_ref), custom_call_target="tpu_custom_call" | custom-call | tf_op jit(solution)/shard_map/attend/pallas_call | solution.py:466
  74.0 13.9 %exchange_3.1 = (bf16[4,128,192]{2,1,0:T(8,128)(2,1)}, bf16[4,128,768]{2,1,0:T(8,128)(2,1)}) custom-call(bf16[4,128,192]{2,1,0:T(8,128)(2,1)} %bitcast.167, bf16[128,768]{1,0:T(8,128)(2,1)} %get-tuple-element.108.refs_1_), custom_call_target="tpu_custom_call" | custom-call | tf_op jit(solution)/shard_map/exchange_3/pallas_call | solution.py:402
  90.1 13.5 %exchange_4.1 = bf16[4,128,768]{2,1,0:T(8,128)(2,1)} custom-call(bf16[4,128,768]{2,1,0:T(8,128)(2,1)} %bitcast.160), custom_call_target="tpu_custom_call" | custom-call | tf_op jit(solution)/shard_map/exchange_4/pallas_call | solution.py:402
  106.0 12.2 %exchange_5.1 = bf16[4,128,768]{2,1,0:T(8,128)(2,1)} custom-call(bf16[128,768]{1,0:T(8,128)(2,1)} %add_convert_fusion.refs_0_), custom_call_target="tpu_custom_call" | custom-call | tf_op jit(solution)/shard_map/exchange_5/pallas_call | solution.py:402
  130.3 5.2 %exchange_16.1 = (bf16[2,768,384]{2,1,0:T(8,128)(2,1)}, bf16[2,768,384]{2,1,0:T(8,128)(2,1)}) custom-call(bf16[768,768]{1,0:T(8,128)(2,1)} %convolution_convert_fusion.1.refs_0_, bf16[768,768]{1,0:T(8,128)(2,1)} %convolution_convert_fusion.refs_1_), custom_call_target="tpu_custom_call" | custom-call | tf_op jit(solution)/shard_map/exchange_16/pallas_call | solution.py:402
  137.9 23.4 %exchange_6.1 = (bf16[4,128,768]{2,1,0:T(8,128)(2,1)}, bf16[4,128,768]{2,1,0:T(8,128)(2,1)}, bf16[4,192,384]{2,1,0:T(8,128)(2,1)}) custom-call(bf16[4,128,768]{2,1,0:T(8,128)(2,1)} %bitcast.171, bf16[4,128,768]{2,1,0:T(8,128)(2,1)} %bitcast.172, bf16[4,192,384]{2,1,0:T(8,128)(2,1)} %bitcast.166), custom_call_target="tpu_custom_call" | custom-call | tf_op jit(solution)/shard_map/exchange_6/pallas_call | solution.py:402
  166.9 17.4 %exchange_7.1 = (bf16[4,128,768]{2,1,0:T(8,128)(2,1)}, bf16[4,4,48,384]{3,2,1,0:T(8,128)(2,1)}) custom-call(bf16[128,768]{1,0:T(8,128)(2,1)} %get-tuple-element.102.refs_0_, bf16[4,4,48,384]{3,2,1,0:T(8,128)(2,1)} %bitcast.162), custom_call_target="tpu_custom_call" | custom-call | tf_op jit(solution)/shard_map/exchange_7/pallas_call | solution.py:402
  191.3 10.4 %exchange_8.1 = (bf16[4,128,192]{2,1,0:T(8,128)(2,1)}, bf16[4,48,384]{2,1,0:T(8,128)(2,1)}, bf16[2,192,384]{2,1,0:T(8,128)(2,1)}) custom-call(bf16[4,128,192]{2,1,0:T(8,128)(2,1)} %bitcast.168, bf16[4,48,384]{2,1,0:T(8,128)(2,1)} %reduce_sum.328.refs_1_, bf16[192,768]{1,0:T(8,128)(2,1)} %fusion.7.refs_2_), custom_call_target="tpu_custom_call" | custom-call | tf_op jit(solution)/shard_map/exchange_8/pallas_call | solution.py:402
  201.7 7.8 %attend_back.1 = (bf16[512,192]{1,0:T(8,128)(2,1)}, bf16[1024,384]{1,0:T(8,128)(2,1)}, f32[1,192]{1,0:T(1,128)}, f32[1,192]{1,0:T(1,128)}) custom-call(bf16[512,576]{1,0:T(8,128)(2,1)} %bitcast.158, bf16[1024,384]{1,0:T(8,128)(2,1)} %bitcast.154, s32[512,1]{1,0:T(8,128)} %fusion.31.qpos_ref, s32[1,1024]{1,0:T(1,128)} %fusion.33.kpos_ref, ...), custom_call_target="tpu_custom_call" | custom-call | tf_op jit(solution)/shard_map/attend_back/pallas_call | solution.py:466
  209.5 3.2 exchange_9.1
  215.9 22.7 %exchange_10.1 = (bf16[4,128,576]{2,1,0:T(8,128)(2,1)}, bf16[4,48,384]{2,1,0:T(8,128)(2,1)}) custom-call(bf16[4,128,576]{2,1,0:T(8,128)(2,1)} %pad_maximum_fusion.refs_0_, bf16[4,48,384]{2,1,0:T(8,128)(2,1)} %bitcast.178), custom_call_target="tpu_custom_call" | custom-call | tf_op jit(solution)/shard_map/exchange_10/pallas_call | solution.py:402
  238.7 3.2 convolution_convert_fusion.4
  246.7 21.5 %exchange_11.1 = (bf16[4,128,768]{2,1,0:T(8,128)(2,1)}, bf16[2,768,288]{2,1,0:T(8,128)(2,1)}, bf16[4,4,48,384]{3,2,1,0:T(8,128)(2,1)}, bf16[4,48,384]{2,1,0:T(8,128)(2,1)}) custom-call(bf16[4,128,768]{2,1,0:T(8,128)(2,1)} %bitcast.173, bf16[2,768,288]{2,1,0:T(8,128)(2,1)} %bitcast.156, bf16[4,48,384]{2,1,0:T(8,128)(2,1)} %get-tuple-element.72.refs_2_, ...), custom_call_target="tpu_custom_call" | custom-call | tf_op jit(solution)/shard_map/exchange_11/pallas_call | solution.py:402
  275.4 17.9 %exchange_12.1 = (bf16[4,4,48,288]{3,2,1,0:T(8,128)(2,1)}, f32[2,72,128]{2,1,0:T(8,128)}, bf16[4,48,3072]{2,1,0:T(8,128)(2,1)}, bf16[4,48,768]{2,1,0:T(8,128)(2,1)}) custom-call(bf16[4,4,48,288]{3,2,1,0:T(8,128)(2,1)} %bitcast.163, f32[72,128]{1,0:T(8,128)} %bitcast.182, bf16[4,4,48,384]{3,2,1,0:T(8,128)(2,1)} %get-tuple-element.78.refs_2_, ...), custom_call_target="tpu_custom_call" | custom-call | tf_op jit(solution)/shard_map/exchange_12/pallas_call | solution.py:402
  297.4 20.5 %exchange_13.1 = (bf16[4,48,288]{2,1,0:T(8,128)(2,1)}, f32[4,72,128]{2,1,0:T(8,128)}, bf16[4,192,384]{2,1,0:T(8,128)(2,1)}) custom-call(bf16[4,48,288]{2,1,0:T(8,128)(2,1)} %reduce_sum.344.refs_0_, f32[72,128]{1,0:T(8,128)} %reduce_sum.345.refs_1_, bf16[192,384]{1,0:T(8,128)(2,1)} %reduce_sum.346.refs_2_), custom_call_target="tpu_custom_call" | custom-call | tf_op jit(solution)/shard_map/exchange_13/pallas_call | solution.py:402
  319.4 17.4 %exchange_14.1 = (bf16[4,4,48,288]{3,2,1,0:T(8,128)(2,1)}, f32[4,72,128]{2,1,0:T(8,128)}, bf16[4,192,768]{2,1,0:T(8,128)(2,1)}) custom-call(bf16[4,48,288]{2,1,0:T(8,128)(2,1)} %get-tuple-element.83.refs_0_, f32[72,128]{1,0:T(8,128)} %reduce_sum.347.refs_1_, bf16[4,1,192,384]{3,2,1,0:T(8,128)(2,1)} %bitcast.177), custom_call_target="tpu_custom_call" | custom-call | tf_op jit(solution)/shard_map/exchange_14/pallas_call | solution.py:402
  338.4 3.4 exchange_15.1
  343.3 3.2 copy.54
  346.5 4.8 %reshape.599 = f32[192,4,3,192]{3,2,1,0:T(4,128)S(1)} reshape(f32[4,48,4,2,288]{4,3,2,1,0:T(2,128)} %copy.54) | data formatting | bytes 3538944 | tf_op jit(solution)/shard_map/convert_element_type | solution.py:681
  353.4 3.8 %reshape.595 = f32[192,2304]{1,0:T(8,128)} reshape(f32[192,3,4,192]{3,2,1,0:T(4,128)} %copy.55) | data formatting | bytes 3538944 | tf_op jit(solution)/shard_map/convert_element_type | solution.py:681
  (140 shorter events, 76.3 us)
Async XLA Ops:
  0.6 120.7 %copy-start = (bf16[768,768]{1,0:T(8,128)(2,1)S(1)}, bf16[768,768]{1,0:T(8,128)(2,1)}, u32[]{:S(2)}) copy-start(bf16[768,768]{1,0:T(8,128)(2,1)} %param.28) | copy-start | bytes 3538948
  7.0 1.9 copy-start.16
  7.0 1.9 copy-start.19
  63.3 10.0 %copy-start.3 = (f32[1,128,768]{2,1,0:T(8,128)S(1)}, f32[1,128,768]{2,1,0:T(8,128)}, u32[]{:S(2)}) copy-start(f32[1,128,768]{2,1,0:T(8,128)} %param.16) | copy-start | bytes 1179652
  66.4 21.5 %copy-start.7 = (bf16[192,768]{1,0:T(8,128)(2,1)S(1)}, bf16[192,768]{1,0:T(8,128)(2,1)}, u32[]{:S(2)}) copy-start(bf16[192,768]{1,0:T(8,128)(2,1)} %param.22) | copy-start | bytes 884740
  90.1 14.8 %copy-start.18 = (f32[768]{0:T(1024)S(1)}, f32[768]{0:T(1024)}, u32[]{:S(2)}) copy-start(f32[768]{0:T(1024)} %param.23) | copy-start | bytes 9220
  103.5 1.7 copy-start.15
  103.6 1.7 copy-start.20
  121.4 2.0 copy-start.26
  126.5 2.0 copy-start.9
  166.9 23.3 %copy-start.8 = (bf16[4,128,192]{2,1,0:T(8,128)(2,1)S(1)}, bf16[4,128,192]{2,1,0:T(8,128)(2,1)}, u32[]{:S(2)}) copy-start(bf16[4,128,192]{2,1,0:T(8,128)(2,1)} %get-tuple-element.57) | copy-start | bytes 589828
  184.3 5.9 %copy-start.4 = (bf16[4,128,768]{2,1,0:T(8,128)(2,1)S(1)}, bf16[4,128,768]{2,1,0:T(8,128)(2,1)}, u32[]{:S(2)}) copy-start(bf16[4,128,768]{2,1,0:T(8,128)(2,1)} %get-tuple-element.65) | copy-start | bytes 2359300
  209.5 4.6 %copy-start.13 = (bf16[512,192]{1,0:T(8,128)(2,1)S(1)}, bf16[512,192]{1,0:T(8,128)(2,1)}, u32[]{:S(2)}) copy-start(bf16[512,192]{1,0:T(8,128)(2,1)} %get-tuple-element.68) | copy-start | bytes 589828
  212.7 2.5 copy-start.12
  238.6 3.2 copy-start.25
  238.6 3.2 copy-start.27
  243.5 2.6 copy-start.14
  246.7 23.2 %copy-start.21 = (f32[768]{0:T(1024)S(1)}, f32[768]{0:T(1024)}, u32[]{:S(2)}) copy-start(f32[768]{0:T(1024)} %param.29) | copy-start | bytes 9220
  271.1 2.8 copy-start.23
  271.1 3.0 copy-start.22
  272.9 23.7 %copy-start.10 = (bf16[4,192,384]{2,1,0:T(8,128)(2,1)S(1)}, bf16[4,192,384]{2,1,0:T(8,128)(2,1)}, u32[]{:S(2)}) copy-start(bf16[4,192,384]{2,1,0:T(8,128)(2,1)} %get-tuple-element.82) | copy-start | bytes 1769476
  353.4 3.8 %copy-start.11 = (bf16[4,48,768]{2,1,0:T(8,128)(2,1)S(1)}, bf16[4,48,768]{2,1,0:T(8,128)(2,1)}, u32[]{:S(2)}) copy-start(bf16[4,48,768]{2,1,0:T(8,128)(2,1)} %get-tuple-element.88) | copy-start | bytes 884740
  353.4 4.7 %copy-start.5 = (bf16[4,48,3072]{2,1,0:T(8,128)(2,1)S(1)}, bf16[4,48,3072]{2,1,0:T(8,128)(2,1)}, u32[]{:S(2)}) copy-start(bf16[4,48,3072]{2,1,0:T(8,128)(2,1)} %get-tuple-element.89) | copy-start | bytes 3538948
  358.0 2.4 copy-start.6
  (4 other events, 5.3 us)
